TPU v7x, 256 devices: a whole 4x4x8 slice. The times are simulated.
256 devices in a mesh: mem: 4 (over y), col: 64 (over z, x, core).
Axes of the slice: x: 4, y: 4, z: 8, core: 2. Of those that a mesh axis runs over, the one named last changes fastest.
Arguments:
- increment: float32 [8, 1048576], P(None, 'col'), may hold values from -6 to 6
- ensemble: bfloat16 [64, 8, 1048576], P('mem', None, 'col'), may hold values from -15 to 15
- climate: float32 [8, 1048576], P(None, 'col'), may hold values from 0.5 to 2
- restrict_dest: int32 [16384, 1], replicated, may hold values from 0 to 63; in each aligned block of 256 rows (0 to 255, 256 to 511, ...) at most 8 rows name the same one
- restrict_local: int32 [16384], replicated, may hold values from 0 to 255
- restrict_weight: float32 [1048576], P('col'), may hold values from 0.05 to 0.2
- conv_blocks: bfloat16 [128, 4, 128, 128], P('col'), may hold values from -0.25 to 0.25
- neighbours: int32 [128, 4], P('col'), may hold values from 0 to 127, as said below
- interp_dest: int32 [16384, 2], replicated, may hold values from 0 to 63, all different within a row; in each aligned block of 256 rows (0 to 255, 256 to 511, ...) at most 16 rows name the same one
- interp_local: int32 [16384, 2], replicated, may hold values from 0 to 255
- interp_weight: float32 [2, 1048576], P(None, 'col'), may hold values from 0.2 to 1
Outputs:
- once_applied: float32 [8, 1048576], P(None, 'col')
- twice_applied: float32 [8, 1048576], P(None, 'col')
Inputs may be any that keep to these rules, and one draw needn't show every extreme that they name: `restrict_dest`: in each aligned block of 256 rows (the tiles of one index of col) no device number appears in more than 8 rows. `interp_dest`: the two entries of a row differ. In each aligned block of 256 rows no device number appears in more than 16 rows. `neighbours`: the 4 entries of row b are distinct blocks among b - 2 to b + 2, taken modulo 128.
All inputs are finite; a program needn't handle non-finite values.
Results may differ from a plain program's by a relative error of at most 0.008.
Values may be sent and summed in bfloat16 or wider, within the bound.
A program may use at most 128 MiB of HBM per device.

v0:
```python
import jax
import jax.numpy as jnp
from jax import lax
from jax.sharding import PartitionSpec as P

TILE = 64


def padded(array, sides, width):
    for axis, dim in sides:
        size, length = (lax.axis_size(axis), array.shape[dim])
        up = [(i, (i + 1) % size) for i in range(size)]
        down = [(j, i) for i, j in up]
        last = lax.slice_in_dim(array, length - width, length, axis=dim)
        leading = lax.slice_in_dim(array, 0, width, axis=dim)
        before = lax.ppermute(last, axis, up)
        after = lax.ppermute(leading, axis, down)
        array = jnp.concatenate([before, array, after], axis=dim)
    return array


def sent_to_all(array, axis):
    copies = jnp.broadcast_to(array, (lax.axis_size(axis), *array.shape))
    return lax.all_to_all(copies, axis, split_axis=0, concat_axis=0, tiled=True)


def taken_together(array, axis):
    everything = sent_to_all(array, axis)
    return jnp.sum(everything, axis=0)


def rank_slots(targets, count_all):
    onehot = (targets[:, None] == jnp.arange(count_all)[None, :]).astype(jnp.int32)
    before = jnp.cumsum(onehot, axis=0) - onehot
    return jnp.sum(before * onehot, axis=1)


def slot_nodes(targets, node_ids, myself, capacity):
    to_me = (targets == myself).astype(jnp.int32)
    before = jnp.cumsum(to_me, axis=1) - to_me
    slot_hits = to_me[:, :, None] * (
        before[:, :, None] == jnp.arange(capacity)[None, None, :]
    ).astype(jnp.int32)
    node_of = jnp.sum(slot_hits * node_ids[:, :, None], axis=1)
    filled = jnp.sum(slot_hits, axis=1)
    return (node_of.reshape(-1), filled.reshape(-1))


def unpack_matrix(node_of, filled, node_count):
    matched = (node_of[None, :] == jnp.arange(node_count)[:, None]) & (filled[None, :] > 0)
    return matched.astype(jnp.float32)


def pair_table(width):
    halves = jnp.arange(2 * width) // width
    return (halves[:, None] == jnp.arange(2)[None, :]).astype(jnp.float32)


def apply_once(
    state,
    ensemble,
    climate,
    restrict_dest,
    restrict_local,
    restrict_weight,
    conv_blocks,
    neighbours,
    interp_dest,
    interp_local,
    interp_weight,
):
    col_count = lax.axis_size("col")
    myself = lax.axis_index("col")
    members_here, levels, fine_local = ensemble.shape
    coarse_local = fine_local // TILE
    block_count = neighbours.shape[0]
    node_block = coarse_local // block_count
    capacity = max(2, 2 * coarse_local // col_count)
    feature = members_here * levels
    halves = pair_table(TILE)
    weighted = state * restrict_weight[None, :]
    product = ensemble.astype(jnp.float32) * weighted[None, :, :]
    paired = product.reshape(feature * (coarse_local // 2), 2 * TILE)
    tile_totals = jnp.dot(paired, halves)
    partial_value = tile_totals.reshape(feature, coarse_local).T
    owner_all = restrict_dest[:, 0].reshape(col_count, coarse_local)
    local_all = restrict_local.reshape(col_count, coarse_local)
    my_owner = lax.dynamic_index_in_dim(owner_all, myself, 0, keepdims=False)
    slot_index = my_owner * capacity + rank_slots(my_owner, col_count)
    packing = (slot_index[None, :] == jnp.arange(col_count * capacity)[:, None]).astype(jnp.float32)
    outgoing = jnp.dot(packing, partial_value).reshape(col_count, capacity, feature)
    incoming = lax.all_to_all(
        outgoing.astype(jnp.bfloat16), "col", split_axis=0, concat_axis=0, tiled=True
    ).astype(outgoing.dtype)
    node_of, filled = slot_nodes(owner_all, local_all, myself, capacity)
    unpack = unpack_matrix(node_of, filled, coarse_local)
    coarse = jnp.dot(unpack, incoming.reshape(-1, feature))
    coarse_half = coarse.astype(jnp.bfloat16)
    extended = padded(coarse_half, (("col", 0),), coarse_local)
    block_total = block_count * col_count
    relative = (neighbours - (myself - 1) * block_count) % block_total
    chooser = (relative[:, :, None] == jnp.arange(3 * block_count)[None, None, :]).astype(
        jnp.bfloat16
    )
    picked = jnp.einsum(
        "bkr,rcm->bkcm",
        chooser,
        extended.reshape(3 * block_count, node_block, feature),
        preferred_element_type=jnp.float32,
    ).astype(jnp.bfloat16)
    convolved = jnp.einsum(
        "bkij,bkjm->bim", conv_blocks, picked, preferred_element_type=jnp.float32
    )
    node_values = convolved.reshape(coarse_local, feature).astype(jnp.bfloat16)
    capacity_pair = 2 * capacity
    targets_pair = interp_dest.reshape(col_count, 2 * coarse_local)
    nodes_pair = interp_local.reshape(col_count, 2 * coarse_local)
    node_of, filled = slot_nodes(targets_pair, nodes_pair, myself, capacity_pair)
    gather_rows = (
        (node_of[:, None] == jnp.arange(coarse_local)[None, :]) & (filled[:, None] > 0)
    ).astype(jnp.bfloat16)
    replies = jnp.dot(gather_rows, node_values, preferred_element_type=jnp.float32).astype(
        jnp.bfloat16
    )
    answers = lax.all_to_all(
        replies.reshape(col_count, capacity_pair, feature),
        "col",
        split_axis=0,
        concat_axis=0,
        tiled=True,
    )
    my_targets = lax.dynamic_index_in_dim(targets_pair, myself, 0, keepdims=False)
    slot_pair = my_targets * capacity_pair + rank_slots(my_targets, col_count)
    chooser_fine = (slot_pair[:, None] == jnp.arange(col_count * capacity_pair)[None, :]).astype(
        jnp.bfloat16
    )
    fetched = jnp.dot(
        chooser_fine, answers.reshape(-1, feature), preferred_element_type=jnp.float32
    )
    fetched_small = fetched.reshape(coarse_local, 2, feature).transpose(1, 2, 0)
    spread = halves.T
    first_value = jnp.dot(
        fetched_small[0].reshape(feature * (coarse_local // 2), 2), spread
    ).reshape(feature, fine_local)
    second_value = jnp.dot(
        fetched_small[1].reshape(feature * (coarse_local // 2), 2), spread
    ).reshape(feature, fine_local)
    interp = first_value * interp_weight[0][None, :] + second_value * interp_weight[1][None, :]
    member_terms = ensemble.reshape(feature, fine_local).astype(jnp.float32) * interp
    local_sum = jnp.sum(member_terms.reshape(members_here, levels, fine_local), axis=0)
    members_all = members_here * lax.axis_size("mem")
    ensemble_sum = taken_together(local_sum, "mem")
    return climate * state + ensemble_sum / (members_all - 1)


def per_device(
    increment,
    ensemble,
    climate,
    restrict_dest,
    restrict_local,
    restrict_weight,
    conv_blocks,
    neighbours,
    interp_dest,
    interp_local,
    interp_weight,
):
    once_applied = apply_once(
        increment,
        ensemble,
        climate,
        restrict_dest,
        restrict_local,
        restrict_weight,
        conv_blocks,
        neighbours,
        interp_dest,
        interp_local,
        interp_weight,
    )
    twice_applied = apply_once(
        once_applied,
        ensemble,
        climate,
        restrict_dest,
        restrict_local,
        restrict_weight,
        conv_blocks,
        neighbours,
        interp_dest,
        interp_local,
        interp_weight,
    )
    return (once_applied, twice_applied)


def solution(mesh):
    in_specs = (
        P(None, "col"),
        P("mem", None, "col"),
        P(None, "col"),
        P(),
        P(),
        P("col"),
        P("col", None, None, None),
        P("col", None),
        P(),
        P(),
        P(None, "col"),
    )
    out_specs = (P(None, "col"), P(None, "col"))
    return jax.shard_map(
        per_device, mesh=mesh, in_specs=in_specs, out_specs=out_specs, check_vma=False
    )
```

profile of v0, /device:TPU:1, one launch (start us, length us, event | category | flops | bytes accessed | tf_op | source)
XLA Modules:
  0.0 377.9 jit_solution(4414855448604255443)
XLA Ops:
  0.7 0.5 broadcast.257
  1.2 1.6 reduce.15
  2.9 0.6 reduce-window.36
  3.9 1.1 broadcast_multiply_fusion.1
  5.0 5.0 %convert_multiply_fusion.3 = bf16[16,8,16384]{2,1,0:T(8,128)(2,1)} fusion(bf16[16,8,16384]{2,1,0:T(8,128)(2,1)} %param.12, f32[8,16384]{1,0:T(8,128)S(1)} %broadcast_multiply_fusion.1), kind=kLoop, calls=%fused_computation.3 | loop fusion | flops 6291456 | bytes 8912896 | tf_op jit(solution)/shard_map/mul | solution.py:82
  10.0 7.4 %reshape.316 = bf16[16384,128]{1,0:T(8,128)(2,1)} reshape(bf16[16,8,16384]{2,1,0:T(8,128)(2,1)} %convert_multiply_fusion.3) | data formatting | bytes 8388608 | tf_op jit(solution)/shard_map/reshape | solution.py:83
  17.4 5.5 %fusion.59 = bf16[16384,2]{1,0:T(8,128)(2,1)} fusion(bf16[16384,128]{1,0:T(8,128)(2,1)} %reshape.316, s32[128]{0:T(128)S(1)} %and_select_fusion), kind=kOutput, calls=%fused_computation.94 | convolution fusion | flops 8388864 | bytes 4260352 | tf_op jit(solution)/shard_map/dot_general | solution.py:84
  22.8 7.2 %reshape.334 = bf16[128,256,1]{1,0,2:T(8,128)(2,1)S(1)} reshape(bf16[16384,2]{1,0:T(8,128)(2,1)} %fusion.59) | data formatting | bytes 131072 | tf_op jit(solution)/shard_map/reshape | solution.py:85
  30.1 0.9 convolution_convert_fusion.5
  31.0 13.4 %all-to-all-start = ((bf16[64,8,128]{2,1,0:T(8,128)(2,1)}), bf16[64,8,128]{2,1,0:T(8,128)(2,1)S(1)}, u32[]{:S(2)}, u32[]{:S(2)}) async-start(bf16[64,8,128]{2,1,0:T(8,128)(2,1)} %convolution_convert_fusion.5), calls=%async_computation | async-start | bytes 262144 | tf_op jit(solution)/shard_map/all_to_all | solution.py:92
  44.6 5.0 %copy.30 = s32[16384,2]{1,0:T(8,128)} copy(s32[16384,2]{0,1:T(2,128)S(1)} %copy-done.4) | data formatting | bytes 262144 | tf_op args[8]
  49.6 0.6 reduce-window.34
  50.5 2.2 select_reduce_fusion.1
  52.9 5.0 %copy.33 = s32[16384,2]{1,0:T(8,128)} copy(s32[16384,2]{0,1:T(2,128)S(1)} %compare_convert_fusion.1) | data formatting | bytes 262144 | tf_op jit(solution)/shard_map/convert_element_type | solution.py:39
  57.9 6.9 %reshape.332 = s32[64,4,128]{2,1,0:T(4,128)S(1)} reshape(s32[16384,2]{1,0:T(8,128)} %copy.33) | data formatting | bytes 262144 | tf_op jit(solution)/shard_map/convert_element_type | solution.py:39
  64.9 1.2 reduce-window.30
  66.4 5.0 %copy.36 = s32[16384,2]{1,0:T(8,128)} copy(s32[16384,2]{0,1:T(2,128)S(1)} %copy-done.6) | data formatting | bytes 262144 | tf_op args[9]
  71.4 6.9 %mul.166 = s32[64,512]{1,0:T(8,128)S(1)} reshape(s32[16384,2]{1,0:T(8,128)} %copy.36) | data formatting | bytes 262144 | tf_op jit(solution)/shard_map/mul | solution.py:44
  78.4 6.9 %reshape.311 = s32[64,512]{1,0:T(8,128)S(1)} reshape(s32[16384,2]{1,0:T(8,128)} %copy.30) | data formatting | bytes 262144 | tf_op jit(solution)/shard_map/reshape | solution.py:116
  85.4 2.2 select_reduce_fusion
  87.9 0.5 copy-done.12
  88.7 0.4 collective-permute-start.1
  89.1 1.9 collective-permute-start
  91.2 1.3 collective-permute-done.1
  92.5 3.0 collective-permute-done
  95.4 0.3 convolution_convert_fusion.3
  96.0 1.2 convolution_convert_fusion.2
  97.1 11.1 %all-to-all-start.1 = ((bf16[64,16,128]{2,1,0:T(8,128)(2,1)}), bf16[64,16,128]{2,1,0:T(8,128)(2,1)S(1)}, u32[]{:S(2)}, u32[]{:S(2)}) async-start(bf16[64,16,128]{2,1,0:T(8,128)(2,1)} %bitcast.19), calls=%async_computation.1 | async-start | bytes 524288 | tf_op jit(solution)/shard_map/all_to_all | solution.py:125
  108.5 1.2 reduce-window.26
  110.3 11.1 %all-to-all-done.1 = bf16[64,16,128]{2,1,0:T(8,128)(2,1)S(1)} async-done(((bf16[64,16,128]{2,1,0:T(8,128)(2,1)}), bf16[64,16,128]{2,1,0:T(8,128)(2,1)S(1)}, u32[]{:S(2)}, u32[]{:S(2)}) %all-to-all-start.1) | async-done | bytes 262176 | tf_op jit(solution)/shard_map/all_to_all | solution.py:125
  121.4 0.5 fusion.8
  122.2 10.0 %reshape_squeeze.18 = bf16[16384,2]{1,0:T(8,128)(2,1)} reshape(bf16[1,128,256]{2,1,0:T(8,128)(2,1)S(1)} %copy.44) | data formatting | bytes 131072 | tf_op jit(solution)/shard_map/reshape;squeeze | solution.py:146
  132.2 10.0 %reshape_squeeze.17 = bf16[16384,2]{1,0:T(8,128)(2,1)} reshape(bf16[1,128,256]{2,1,0:T(8,128)(2,1)S(1)} %copy.43) | data formatting | bytes 131072 | tf_op jit(solution)/shard_map/reshape;squeeze | solution.py:143
  142.3 6.7 %fusion.58 = f32[16384,128]{1,0:T(8,128)} fusion(bf16[16384,2]{1,0:T(8,128)(2,1)} %reshape_squeeze.17, s32[128]{0:T(128)S(1)} %and_select_fusion), kind=kOutput, calls=%fused_computation.93 | convolution fusion | flops 8388864 | bytes 8454656 | tf_op jit(solution)/shard_map/dot_general | solution.py:142
  149.0 9.4 %reshape.322 = f32[16,8,16384]{2,1,0:T(8,128)} reshape(f32[16384,128]{1,0:T(8,128)} %fusion.58) | data formatting | bytes 16777216 | tf_op jit(solution)/shard_map/reshape | solution.py:144
  158.4 6.7 %fusion.57 = f32[16384,128]{1,0:T(8,128)} fusion(bf16[16384,2]{1,0:T(8,128)(2,1)} %reshape_squeeze.18, s32[128]{0:T(128)S(1)} %and_select_fusion), kind=kOutput, calls=%fused_computation.92 | convolution fusion | flops 8388864 | bytes 8454656 | tf_op jit(solution)/shard_map/dot_general | solution.py:145
  165.1 9.4 %reshape.323 = f32[16,8,16384]{2,1,0:T(8,128)} reshape(f32[16384,128]{1,0:T(8,128)} %fusion.57) | data formatting | bytes 16777216 | tf_op jit(solution)/shard_map/reshape | solution.py:147
  174.5 8.0 %fusion = f32[8,16384]{1,0:T(8,128)S(1)} fusion(bf16[16,8,16384]{2,1,0:T(8,128)(2,1)} %param.12, f32[16,8,16384]{2,1,0:T(8,128)} %reshape.323, f32[16,8,16384]{2,1,0:T(8,128)} %reshape.322, f32[16384]{0:T(1024)S(1)} %bitcast.132, f32[16384]{0:T(1024)S(1)} %bitcast.130), kind=kLoop, calls=%fused_computation.4 | loop fusion | flops 12451840 | bytes 21626880 | tf_op jit(solution)/shard_map/reduce_sum | solution.py:150
  182.7 30.2 %all_to_all.30 = f32[4,8,16384]{2,1,0:T(8,128)S(1)} all-to-all(f32[4,8,16384]{2,1,0:T(8,128)S(1)} %broadcast_in_dim.4), channel_id=1, replica_groups=mesh['mem'=4,'col'=64] {'mem'}, dimensions={0} | all-to-all | bytes 4194304 | tf_op jit(solution)/shard_map/all_to_all | solution.py:24
  212.9 0.9 reduce_sum.111
  213.8 2.0 broadcast_multiply_fusion
  215.8 5.0 %convert_multiply_fusion.1 = bf16[16,8,16384]{2,1,0:T(8,128)(2,1)} fusion(bf16[16,8,16384]{2,1,0:T(8,128)(2,1)} %param.12, f32[8,16384]{1,0:T(8,128)S(1)} %get-tuple-element.6), kind=kLoop, calls=%fused_computation.1 | loop fusion | flops 6291456 | bytes 8912896 | tf_op jit(solution)/shard_map/mul | solution.py:82
  220.8 7.4 %reshape.324 = bf16[16384,128]{1,0:T(8,128)(2,1)} reshape(bf16[16,8,16384]{2,1,0:T(8,128)(2,1)} %convert_multiply_fusion.1) | data formatting | bytes 8388608 | tf_op jit(solution)/shard_map/reshape | solution.py:83
  228.2 5.5 %fusion.56 = bf16[16384,2]{1,0:T(8,128)(2,1)} fusion(bf16[16384,128]{1,0:T(8,128)(2,1)} %reshape.324, s32[128]{0:T(128)S(1)} %and_select_fusion), kind=kOutput, calls=%fused_computation.91 | convolution fusion | flops 8388864 | bytes 4260352 | tf_op jit(solution)/shard_map/dot_general | solution.py:84
  233.7 7.2 %reshape.339 = bf16[128,256,1]{1,0,2:T(8,128)(2,1)S(1)} reshape(bf16[16384,2]{1,0:T(8,128)(2,1)} %fusion.56) | data formatting | bytes 131072 | tf_op jit(solution)/shard_map/reshape | solution.py:85
  240.9 0.3 convolution_convert_fusion.4
  241.1 16.5 %all_to_all.31 = bf16[64,8,128]{2,1,0:T(8,128)(2,1)S(1)} all-to-all(bf16[64,8,128]{2,1,0:T(8,128)(2,1)S(1)} %convolution_convert_fusion.4), channel_id=1, replica_groups=mesh['mem'=4,'col'=64] {'col'}, dimensions={0} | all-to-all | bytes 262144 | tf_op jit(solution)/shard_map/all_to_all | solution.py:92
  257.9 0.5 collective-permute-start.3
  258.3 1.4 collective-permute-start.2
  259.7 1.9 collective-permute-done.3
  261.7 0.3 convolution_convert_fusion.1
  262.2 0.5 convolution_convert_fusion
  262.6 22.3 %all_to_all.32 = bf16[64,16,128]{2,1,0:T(8,128)(2,1)S(1)} all-to-all(bf16[64,16,128]{2,1,0:T(8,128)(2,1)S(1)} %bitcast.135), channel_id=1, replica_groups=mesh['mem'=4,'col'=64] {'col'}, dimensions={0} | all-to-all | bytes 524288 | tf_op jit(solution)/shard_map/all_to_all | solution.py:125
  284.9 0.5 fusion.11
  285.7 10.0 %reshape_squeeze.20 = bf16[16384,2]{1,0:T(8,128)(2,1)} reshape(bf16[1,128,256]{2,1,0:T(8,128)(2,1)S(1)} %copy.49) | data formatting | bytes 131072 | tf_op jit(solution)/shard_map/reshape;squeeze | solution.py:146
  295.7 10.0 %reshape_squeeze.19 = bf16[16384,2]{1,0:T(8,128)(2,1)} reshape(bf16[1,128,256]{2,1,0:T(8,128)(2,1)S(1)} %copy.48) | data formatting | bytes 131072 | tf_op jit(solution)/shard_map/reshape;squeeze | solution.py:143
  305.7 6.7 %fusion.55 = f32[16384,128]{1,0:T(8,128)} fusion(bf16[16384,2]{1,0:T(8,128)(2,1)} %reshape_squeeze.19, s32[128]{0:T(128)S(1)} %and_select_fusion), kind=kOutput, calls=%fused_computation.90 | convolution fusion | flops 8388864 | bytes 8454656 | tf_op jit(solution)/shard_map/dot_general | solution.py:142
  312.5 9.4 %reshape.330 = f32[16,8,16384]{2,1,0:T(8,128)} reshape(f32[16384,128]{1,0:T(8,128)} %fusion.55) | data formatting | bytes 16777216 | tf_op jit(solution)/shard_map/reshape | solution.py:144
  321.8 6.7 %fusion.54 = f32[16384,128]{1,0:T(8,128)} fusion(bf16[16384,2]{1,0:T(8,128)(2,1)} %reshape_squeeze.20, s32[128]{0:T(128)S(1)} %and_select_fusion), kind=kOutput, calls=%fused_computation.89 | convolution fusion | flops 8388864 | bytes 8454656 | tf_op jit(solution)/shard_map/dot_general | solution.py:145
  328.6 9.4 %reshape.331 = f32[16,8,16384]{2,1,0:T(8,128)} reshape(f32[16384,128]{1,0:T(8,128)} %fusion.54) | data formatting | bytes 16777216 | tf_op jit(solution)/shard_map/reshape | solution.py:147
  337.9 8.0 %fusion.1 = f32[8,16384]{1,0:T(8,128)S(1)} fusion(bf16[16,8,16384]{2,1,0:T(8,128)(2,1)} %param.12, f32[16,8,16384]{2,1,0:T(8,128)} %reshape.331, f32[16,8,16384]{2,1,0:T(8,128)} %reshape.330, f32[16384]{0:T(1024)S(1)} %bitcast.133, f32[16384]{0:T(1024)S(1)} %bitcast.131), kind=kLoop, calls=%fused_computation.5 | loop fusion | flops 12451840 | bytes 21626880 | tf_op jit(solution)/shard_map/reduce_sum | solution.py:150
  346.1 28.6 %all_to_all.33 = f32[4,8,16384]{2,1,0:T(8,128)S(1)} all-to-all(f32[4,8,16384]{2,1,0:T(8,128)S(1)} %broadcast_in_dim.5), channel_id=1, replica_groups=mesh['mem'=4,'col'=64] {'mem'}, dimensions={0} | all-to-all | bytes 4194304 | tf_op jit(solution)/shard_map/all_to_all | solution.py:24
  374.8 0.9 reduce_sum.129
  375.7 1.9 multiply_add_fusion
  (99 shorter events, 4.3 us)
Async XLA Ops:
  0.6 95.1 %copy-start = (bf16[2,4,128,128]{3,2,1,0:T(8,128)(2,1)S(1)}, bf16[2,4,128,128]{3,2,1,0:T(8,128)(2,1)}, u32[]{:S(2)}) copy-start(bf16[2,4,128,128]{3,2,1,0:T(8,128)(2,1)} %param.17) | copy-start | bytes 786436
  0.7 29.4 %copy-start.9 = (s32[64,8]{1,0:T(8,128)}, s32[64,8]{1,0:T(8,128)S(1)}, u32[]{:S(2)}) copy-start(s32[64,8]{1,0:T(8,128)S(1)} %multiply_add_fusion.2) | copy-start | bytes 6148
  3.9 26.2 %copy-start.14 = (s32[1,256]{1,0:T(1,128)}, s32[1,256]{1,0:T(1,128)S(1)}, u32[]{:S(2)}) copy-start(s32[1,256]{1,0:T(1,128)S(1)} %multiply_add_fusion.3) | copy-start | bytes 3076
  22.8 21.6 %copy-start.5 = (s32[16384,1]{0,1:T(1,128)S(1)}, s32[16384,1]{0,1:T(1,128)}, u32[]{:S(2)}) copy-start(s32[16384,1]{0,1:T(1,128)} %param.14) | copy-start | bytes 196612
  22.8 21.7 %copy-start.4 = (s32[16384,2]{0,1:T(2,128)S(1)}, s32[16384,2]{0,1:T(2,128)}, u32[]{:S(2)}) copy-start(s32[16384,2]{0,1:T(2,128)} %param.19) | copy-start | bytes 393220
  31.0 56.9 %all-to-all-start = ((bf16[64,8,128]{2,1,0:T(8,128)(2,1)}), bf16[64,8,128]{2,1,0:T(8,128)(2,1)S(1)}, u32[]{:S(2)}, u32[]{:S(2)}) async-start(bf16[64,8,128]{2,1,0:T(8,128)(2,1)} %convolution_convert_fusion.5), calls=%async_computation | async-start | bytes 262144 | tf_op jit(solution)/shard_map/all_to_all | solution.py:92
  44.6 5.0 %copy-start.8 = (s32[16384]{0:T(1024)S(1)}, s32[16384]{0:T(1024)}, u32[]{:S(2)}) copy-start(s32[16384]{0:T(1024)} %param.15) | copy-start | bytes 196612
  44.6 8.2 %copy-start.7 = (f32[2,16384]{1,0:T(2,128)S(1)}, f32[2,16384]{1,0:T(2,128)}, u32[]{:S(2)}) copy-start(f32[2,16384]{1,0:T(2,128)} %param.21) | copy-start | bytes 393220
  57.9 8.4 %copy-start.6 = (s32[16384,2]{0,1:T(2,128)S(1)}, s32[16384,2]{0,1:T(2,128)}, u32[]{:S(2)}) copy-start(s32[16384,2]{0,1:T(2,128)} %param.20) | copy-start | bytes 393220
  66.4 5.0 %copy-start.11 = (s32[64,5]{0,1:T(8,128)}, s32[64,5]{0,1:T(8,128)S(1)}, u32[]{:S(2)}) copy-start(s32[64,5]{0,1:T(8,128)S(1)} %reduce-window.31) | copy-start | bytes 3844
  78.3 7.0 %slice-start = ((s32[64,5]{0,1:T(8,128)}), s32[64,4]{0,1:T(4,128)S(1)}, s32[]{:S(2)}) async-start(s32[64,5]{0,1:T(8,128)} %copy-done.11), calls=%async_computation.6 | async-start | bytes 4096 | tf_op jit(solution)/shard_map/slice.3
  78.3 12.7 %copy-start.18 = (s32[2,4]{1,0:T(2,128)S(1)}, s32[2,4]{1,0:T(2,128)}, u32[]{:S(2)}) copy-start(s32[2,4]{1,0:T(2,128)} %param.18) | copy-start | bytes 100
  87.8 44.5 %copy-start.19 = (pred[512]{0:T(512)(128)(4,1)}, pred[512]{0:T(512)(128)(4,1)S(1)}, u32[]{:S(2)}) copy-start(pred[512]{0:T(512)(128)(4,1)S(1)} %gt.27) | copy-start | bytes 1540
  87.9 0.6 copy-start.12
  88.7 3.8 collective-permute-start.1
  89.1 6.3 %collective-permute-start = (bf16[256,128]{1,0:T(8,128)(2,1)S(1)}, bf16[256,128]{1,0:T(8,128)(2,1)S(1)}, u32[]{:S(2)}, u32[]{:S(2)}) collective-permute-start(bf16[256,128]{1,0:T(8,128)(2,1)S(1)} %convolution_convert_fusion.7), channel_id=1, source_target_pairs={{0,1},{1,2},{2,3},{3,4},{4,5},{5,6},{6,7},{7,8},{8,9},{9,10},{10,1... | collective-permute-start | bytes 196616 | tf_op jit(solution)/shard_map/ppermute | solution.py:16
  91.1 6.0 %copy-start.16 = (pred[1024]{0:T(1024)(128)(4,1)}, pred[1024]{0:T(1024)(128)(4,1)S(1)}, u32[]{:S(2)}) copy-start(pred[1024]{0:T(1024)(128)(4,1)S(1)} %gt.25) | copy-start | bytes 3076
  97.1 24.3 %all-to-all-start.1 = ((bf16[64,16,128]{2,1,0:T(8,128)(2,1)}), bf16[64,16,128]{2,1,0:T(8,128)(2,1)S(1)}, u32[]{:S(2)}, u32[]{:S(2)}) async-start(bf16[64,16,128]{2,1,0:T(8,128)(2,1)} %bitcast.19), calls=%async_computation.1 | async-start | bytes 524288 | tf_op jit(solution)/shard_map/all_to_all | solution.py:125
  182.5 31.3 %copy-start.1 = (f32[8,16384]{1,0:T(8,128)S(1)}, f32[8,16384]{1,0:T(8,128)}, u32[]{:S(2)}) copy-start(f32[8,16384]{1,0:T(8,128)} %param.11) | copy-start | bytes 1572868
  182.5 31.3 %copy-start.2 = (f32[8,16384]{1,0:T(8,128)S(1)}, f32[8,16384]{1,0:T(8,128)}, u32[]{:S(2)}) copy-start(f32[8,16384]{1,0:T(8,128)} %param.13) | copy-start | bytes 1572868
  233.6 7.2 %copy-start.10 = (s32[64,8]{1,0:T(8,128)S(1)}, s32[64,8]{1,0:T(8,128)}, u32[]{:S(2)}) copy-start(s32[64,8]{1,0:T(8,128)} %copy-done.9) | copy-start | bytes 6148
  233.6 7.2 %copy-start.15 = (s32[1,256]{1,0:T(1,128)S(1)}, s32[1,256]{1,0:T(1,128)}, u32[]{:S(2)}) copy-start(s32[1,256]{1,0:T(1,128)} %copy-done.14) | copy-start | bytes 3076
  233.6 24.0 %copy-start.13 = (s32[512]{0:T(512)S(1)}, s32[512]{0:T(512)}, u32[]{:S(2)}) copy-start(s32[512]{0:T(512)} %copy-done.12) | copy-start | bytes 6148
  233.6 24.0 %copy-start.20 = (pred[512]{0:T(512)(128)(4,1)S(1)}, pred[512]{0:T(512)(128)(4,1)}, u32[]{:S(2)}) copy-start(pred[512]{0:T(512)(128)(4,1)} %copy-done.19) | copy-start | bytes 1540
  233.6 28.5 %copy-start.17 = (pred[1024]{0:T(1024)(128)(4,1)S(1)}, pred[1024]{0:T(1024)(128)(4,1)}, u32[]{:S(2)}) copy-start(pred[1024]{0:T(1024)(128)(4,1)} %copy-done.16) | copy-start | bytes 3076
  257.9 3.8 collective-permute-start.3
  258.3 3.3 collective-permute-start.2
  346.0 29.7 %copy-start.3 = (f32[8,16384]{1,0:T(8,128)S(1)}, f32[8,16384]{1,0:T(8,128)}, u32[]{:S(2)}) copy-start(f32[8,16384]{1,0:T(8,128)} %get-tuple-element.7) | copy-start | bytes 1572868
where the time goes:
time: 384 us; the launch traced here: 378 us
  local copies, waits for them, and re-layouts  146 us (38%)
  blocking collectives  97.6 us (25%)
  other arithmetic  43.5 us (11%)
  matrix products  43.2 us (11%)
  starting transfers between devices  28.7 us (7%)
  waiting for transfers between devices  17.3 us (5%)
    all_to_all x2, blocking collectives, sent_to_all(): return lax.all_to_all(copies, axis, split_axis=0, concat_axis=0, tiled=True)  58.8 us
    all_to_all x1, blocking collectives, apply_once(): lax.all_to_all(replies.reshape(col_count, capacity_pair, feature), 'col',...  22.3 us
    another operation x2, local copies, waits for them, and re-layouts, apply_once(): fetched_small[1].reshape(feature * (coarse_local // 2), 2)  20.1 us
    another operation x2, local copies, waits for them, and re-layouts, apply_once(): fetched_small[0].reshape(feature * (coarse_local // 2), 2)  20 us
    reshape x2, local copies, waits for them, and re-layouts, apply_once(): first_value = jnp.dot(fetched_small[0].reshape(feature * (coarse_local //...  18.8 us
    reshape x2, local copies, waits for them, and re-layouts, apply_once(): second_value = jnp.dot(fetched_small[1].reshape(feature * (coarse_local /...  18.8 us
    all_to_all x1, blocking collectives, apply_once(): lax.all_to_all(outgoing.astype(jnp.bfloat16), 'col', split_axis=0, concat...  16.5 us
    reduce_sum x2, other arithmetic, apply_once(): jnp.sum(member_terms.reshape(members_here, levels, fine_local), axis=0)  16.1 us
  transfers between devices with their start and end apart: 6, of which 4 were waited for; matrix products, arithmetic and copies ran while one was open for 12% of the time, Pallas kernels for 0%

commit v1 on v0

v1 whole, which is shorter than its diff:
```python
import functools

import jax
import jax.numpy as jnp
from jax import lax
from jax.experimental import pallas as pl
from jax.experimental.pallas import tpu as pltpu
from jax.sharding import PartitionSpec as P

TILE = 64
CHUNK = 1024
F32 = jnp.float32
BF16 = jnp.bfloat16
MESH = pl.DeviceIdType.MESH


def iota(shape, dim):
    return lax.broadcasted_iota(jnp.int32, shape, dim)


def dot(a, b):
    return jnp.dot(a, b, preferred_element_type=F32)


def dot_tn(a, b):
    return lax.dot_general(a, b, (((0,), (0,)), ((), ())), preferred_element_type=F32)


def ones_where(mask):
    return jnp.where(mask, 1.0, 0.0).astype(BF16)


def kernel(
    cfg,
    neigh_ref,
    inc_ref,
    ens_hbm,
    clim_hbm,
    rd_ref,
    rl_ref,
    rw_ref,
    conv_hbm,
    id_ref,
    il_ref,
    iw_ref,
    once_hbm,
    twice_hbm,
    ens_ref,
    clim_ref,
    conv_ref,
    once_ref,
    twice_ref,
    sum_ref,
    spread_ref,
    pack_ref,
    unpack_ref,
    gather_ref,
    choose_ref,
    partial_ref,
    value_ref,
    a1_send,
    a1_recv,
    ext_first,
    ext_second,
    a2_send,
    a2_recv,
    rs_send,
    rs_recv,
    own_ref,
    ag_send,
    ag_recv,
    in_sem,
    out_sem,
    a1_ssem,
    a1_rsem,
    halo_ssem,
    halo_rsem,
    a2_ssem,
    a2_rsem,
    rs_ssem,
    rs_rsem,
    ag_ssem,
    ag_rsem,
):
    n_col, n_mem, members, levels, fine, cap, scale = cfg
    tiles = fine // TILE
    feature = members * levels
    part = fine // n_mem
    part_tiles = part // TILE
    cap2 = 2 * cap
    slots1 = n_col * cap
    slots2 = n_col * cap2
    me = lax.axis_index("col")
    my_mem = lax.axis_index("mem")
    right = lax.rem(me + 1, n_col)
    left = lax.rem(me + n_col - 1, n_col)

    def ens_load(q):
        cols = pl.ds(q * part, part)
        return pltpu.make_async_copy(
            ens_hbm.at[:, :, cols], ens_ref.at[:, :, cols], in_sem.at[q]
        )

    for q in range(n_mem):
        ens_load(q).start()
    clim_load = pltpu.make_async_copy(clim_hbm, clim_ref, in_sem.at[n_mem])
    clim_load.start()
    conv_load = pltpu.make_async_copy(conv_hbm, conv_ref, in_sem.at[n_mem + 1])
    conv_load.start()

    barrier = pltpu.get_barrier_semaphore()

    @pl.loop(1, n_col)
    def _(i):
        pl.semaphore_signal(
            barrier, inc=1, device_id=(my_mem, lax.rem(me + i, n_col)), device_id_type=MESH
        )

    for i in range(1, n_mem):
        pl.semaphore_signal(
            barrier, inc=1, device_id=(lax.rem(my_mem + i, n_mem), me), device_id_type=MESH
        )

    rows = 512

    @pl.loop(0, part // rows)
    def _(c):
        r = iota((rows, 128), 0) + c * rows
        at = pl.ds(pl.multiple_of(c * rows, rows), rows)
        sum_ref[at, :] = ones_where((r >> 6) == iota((rows, 128), 1))

    owner = rd_ref[pl.ds(me, 1), :]
    slot_row = iota((slots1, tiles), 0)
    named = slot_row // cap == owner
    before = dot(
        ones_where(named), ones_where(iota((tiles, tiles), 0) < iota((tiles, tiles), 1))
    )
    pack_ref[...] = ones_where(named & (before == (slot_row % cap).astype(F32)))

    def restrict(state_ref, q):
        base = q * part

        def body(c, acc):
            off = pl.multiple_of(base + c * CHUNK, CHUNK)
            cols = pl.ds(off, CHUNK)
            w = state_ref[:, cols] * rw_ref[:, cols]
            prod = jnp.concatenate(
                [ens_ref[m, :, cols].astype(F32) * w for m in range(members)], axis=0
            ).astype(BF16)
            at = pl.ds(pl.multiple_of(c * CHUNK, CHUNK), CHUNK)
            return acc + dot(prod, sum_ref[at, :])

        acc = lax.fori_loop(0, part // CHUNK, body, jnp.zeros((feature, 128), F32))
        partial_ref[q] = acc.T[:part_tiles].astype(BF16)

    def all_to_all(src, dst, ssem, rsem):
        @pl.loop(1, n_col)
        def _(i):
            peer = lax.rem(me + i, n_col)
            pltpu.make_async_remote_copy(
                src_ref=src.at[peer],
                dst_ref=dst.at[me],
                send_sem=ssem,
                recv_sem=rsem,
                device_id=(my_mem, peer),
                device_id_type=MESH,
            ).start()

        dst[me] = src[me]

    def wait_blocks(ref, sem):
        some = ref.at[pl.ds(0, n_col - 1)]
        pltpu.make_async_copy(some, some, sem).wait()

    def build_unpack():
        spread = ones_where(iota((n_col, slots1), 0) == iota((n_col, slots1), 1) // cap)
        mine = dot_tn(ones_where(rd_ref[...] == me), spread)
        local = dot_tn(rl_ref[...].astype(F32).astype(BF16), spread)
        before = dot(
            ones_where(iota((tiles, tiles), 1) < iota((tiles, tiles), 0)), mine.astype(BF16)
        )
        slot = (iota((tiles, slots1), 1) % cap).astype(F32)
        hit = jnp.where(before == slot, mine, 0.0)
        node = jnp.sum(hit * local, axis=0, keepdims=True)
        filled = jnp.sum(hit, axis=0, keepdims=True)
        node = jnp.where(filled > 0.5, node, -1.0)
        unpack_ref[...] = ones_where(iota((tiles, slots1), 0).astype(F32) == node)

    def build_gather():
        width = 256
        pairs = 2 * tiles
        mask = ones_where(id_ref[...] == me)
        nodes = il_ref[...].astype(F32).astype(BF16)
        lower = ones_where(iota((pairs, pairs), 1) < iota((pairs, pairs), 0))
        for b in range(slots2 // width):
            column = iota((n_col, width), 1) + b * width
            spread = ones_where(iota((n_col, width), 0) == column // cap2)
            mine = dot_tn(mask, spread)
            local = dot_tn(nodes, spread)
            before = dot(lower, mine.astype(BF16))
            slot = ((iota((pairs, width), 1) + b * width) % cap2).astype(F32)
            hit = jnp.where(before == slot, mine, 0.0)
            node = jnp.sum(hit * local, axis=0, keepdims=True)
            filled = jnp.sum(hit, axis=0, keepdims=True)
            node = jnp.where(filled > 0.5, node, -1.0)
            block = jnp.where(iota((tiles, width), 0).astype(F32) == node, 1.0, 0.0)
            gather_ref[pl.ds(b * width, width), :] = block.T.astype(BF16)

    def build_choose():
        width = 256
        pairs = 2 * tiles
        target = id_ref[pl.ds(me, 1), :]
        upper = ones_where(iota((pairs, pairs), 0) < iota((pairs, pairs), 1))
        for b in range(slots2 // width):
            slot_row = iota((width, pairs), 0) + b * width
            named = slot_row // cap2 == target
            before = dot(ones_where(named), upper)
            block = jnp.where(
                named & (before == (slot_row % cap2).astype(F32)), 1.0, 0.0
            )
            choose_ref[:, pl.ds(b * width, width)] = block.T.astype(BF16)

    def build_spread():
        per = part // CHUNK

        @pl.loop(0, n_mem * per)
        def _(i):
            q = i // per
            c = lax.rem(i, per)
            local = pl.ds(pl.multiple_of(c * CHUNK, CHUNK), CHUNK)
            cols = pl.ds(pl.multiple_of(i * CHUNK, CHUNK), CHUNK)
            shape = (part_tiles, CHUNK)
            mask = ((iota(shape, 1) + c * CHUNK) >> 6) == iota(shape, 0)
            for k in range(2):
                spread_ref[q, pl.ds(k * part_tiles, part_tiles), local] = jnp.where(
                    mask, iw_ref[pl.ds(k, 1), cols], 0.0
                ).astype(BF16)

    def member_sum(q, c):
        off = pl.multiple_of(c * CHUNK, CHUNK)
        interp = dot(value_ref[q], spread_ref[q, :, pl.ds(off, CHUNK)])
        cols = pl.ds(pl.multiple_of(q * part + off, CHUNK), CHUNK)
        total = ens_ref[0, :, cols].astype(F32) * interp[0:levels]
        for m in range(1, members):
            total += ens_ref[m, :, cols].astype(F32) * interp[m * levels : (m + 1) * levels]
        return total

    def result_store(ref, hbm, q, sem):
        cols = pl.ds(pl.multiple_of(q * part, part), part)
        return pltpu.make_async_copy(ref.at[:, cols], hbm.at[:, cols], sem)

    for app in range(2):
        state_ref = inc_ref if app == 0 else once_ref
        new_ref, new_hbm = (once_ref, once_hbm) if app == 0 else (twice_ref, twice_hbm)
        if app == 0:
            for q in range(n_mem):
                ens_load(q).wait()
                restrict(state_ref, q)
        outgoing = dot(pack_ref[...], partial_ref[...].reshape(tiles, feature))
        a1_send[app] = outgoing.reshape(n_col, cap, feature).astype(BF16)
        if app == 0:
            pl.semaphore_wait(barrier, n_col - 1 + n_mem - 1)
        all_to_all(a1_send.at[app], a1_recv.at[app], a1_ssem.at[app], a1_rsem.at[app])
        if app == 0:
            build_unpack()
        wait_blocks(a1_recv.at[app], a1_rsem.at[app])
        ext_ref = ext_first if app == 0 else ext_second
        incoming = a1_recv[app].astype(F32).reshape(slots1, feature).astype(BF16)
        coarse = dot(unpack_ref[...], incoming).astype(BF16)
        ext_ref[2:4] = coarse.reshape(2, tiles // 2, feature)
        halos = []
        for side, peer, at in ((0, right, 0), (1, left, 4)):
            halo = pltpu.make_async_remote_copy(
                src_ref=ext_ref.at[pl.ds(2, 2)],
                dst_ref=ext_ref.at[pl.ds(at, 2)],
                send_sem=halo_ssem.at[app, side],
                recv_sem=halo_rsem.at[app, side],
                device_id=(my_mem, peer),
                device_id_type=MESH,
            )
            halo.start()
            halos.append(halo)
        if app == 0:
            build_gather()
            conv_load.wait()
        for halo in halos:
            halo.wait_recv()
        nodes = []
        for b in range(2):
            total = None
            for k in range(4):
                block = lax.rem(
                    neigh_ref[b, k] - (me - 1) * 2 + 4 * n_col, 2 * n_col
                )
                term = dot(conv_ref[b, k], ext_ref[jnp.minimum(block, 5)])
                total = term if total is None else total + term
            nodes.append(total.astype(BF16))
        replies = dot(gather_ref[...], jnp.concatenate(nodes, axis=0))
        a2_send[app] = replies.astype(BF16).reshape(n_col, cap2, feature)
        all_to_all(a2_send.at[app], a2_recv.at[app], a2_ssem.at[app], a2_rsem.at[app])
        if app == 0:
            build_choose()
            build_spread()
            clim_load.wait()
        wait_blocks(a2_recv.at[app], a2_rsem.at[app])
        answers = a2_recv[app].reshape(slots2, feature)
        fetched = dot(choose_ref[...], answers)
        for q in range(n_mem):
            at = q * 2 * part_tiles
            value_ref[q] = fetched[at : at + 2 * part_tiles].T.astype(BF16)

        scatters = []
        for i in (2, 1, 3):
            q = lax.rem(my_mem + i, n_mem)

            @pl.loop(0, part // CHUNK)
            def _(c, i=i, q=q):
                at = pl.ds(pl.multiple_of(c * CHUNK, CHUNK), CHUNK)
                rs_send[app, i - 1, :, at] = member_sum(q, c).astype(BF16)

            copy = pltpu.make_async_remote_copy(
                src_ref=rs_send.at[app, i - 1],
                dst_ref=rs_recv.at[app, i - 1],
                send_sem=rs_ssem.at[app, i - 1],
                recv_sem=rs_rsem.at[app, i - 1],
                device_id=(q, me),
                device_id_type=MESH,
            )
            copy.start()
            scatters.append(copy)

        @pl.loop(0, part // CHUNK)
        def _(c):
            at = pl.ds(pl.multiple_of(c * CHUNK, CHUNK), CHUNK)
            own_ref[:, at] = member_sum(my_mem, c)

        for copy in scatters:
            copy.wait_recv()
        total = own_ref[...]
        for i in range(n_mem - 1):
            total += rs_recv[app, i].astype(F32)
        ag_send[app] = total.astype(BF16)
        gathers = {}
        for i in (2, 1, 3):
            copy = pltpu.make_async_remote_copy(
                src_ref=ag_send.at[app],
                dst_ref=ag_recv.at[app, i - 1],
                send_sem=ag_ssem.at[app, i - 1],
                recv_sem=ag_rsem.at[app, i - 1],
                device_id=(lax.rem(my_mem + i, n_mem), me),
                device_id_type=MESH,
            )
            copy.start()
            gathers[i] = copy
        for i in (0, 1, 3, 2):
            q = lax.rem(my_mem + n_mem - i, n_mem)
            if i:
                gathers[i].wait_recv()
                summed = ag_recv[app, i - 1]
            else:
                summed = ag_send[app]
            cols = pl.ds(pl.multiple_of(q * part, part), part)
            new_ref[:, cols] = (
                clim_ref[:, cols] * state_ref[:, cols] + summed.astype(F32) * scale
            )
            result_store(new_ref, new_hbm, q, out_sem.at[app, i]).start()
            if app == 0:
                restrict(new_ref, q)
        for copy in scatters:
            copy.wait_send()
        for copy in gathers.values():
            copy.wait_send()
        for halo in halos:
            halo.wait_send()

    for app in range(2):
        wait_blocks(a1_send.at[app], a1_ssem.at[app])
        wait_blocks(a2_send.at[app], a2_ssem.at[app])
        new_ref, new_hbm = (once_ref, once_hbm) if app == 0 else (twice_ref, twice_hbm)
        for i in range(n_mem):
            q = lax.rem(my_mem + n_mem - i, n_mem)
            result_store(new_ref, new_hbm, q, out_sem.at[app, i]).wait()


def per_device(
    increment,
    ensemble,
    climate,
    restrict_dest,
    restrict_local,
    restrict_weight,
    conv_blocks,
    neighbours,
    interp_dest,
    interp_local,
    interp_weight,
):
    n_col = lax.axis_size("col")
    n_mem = lax.axis_size("mem")
    members, levels, fine = ensemble.shape
    tiles = fine // TILE
    part = fine // n_mem
    part_tiles = part // TILE
    feature = members * levels
    cap = max(2, 2 * tiles // n_col)
    scale = 1.0 / (members * n_mem - 1)
    cfg = (n_col, n_mem, members, levels, fine, cap, scale)

    def pairs(a):
        a = a.reshape(n_col, n_mem, part_tiles, 2)
        return a.transpose(0, 1, 3, 2).reshape(n_col, 2 * tiles)

    vmem = pl.BlockSpec(memory_space=pltpu.VMEM)
    smem = pl.BlockSpec(memory_space=pltpu.SMEM)
    hbm = pl.BlockSpec(memory_space=pl.ANY)
    dma = pltpu.SemaphoreType.DMA
    result = jax.ShapeDtypeStruct((levels, fine), F32)
    return pl.pallas_call(
        functools.partial(kernel, cfg),
        out_shape=(result, result),
        in_specs=[smem, vmem, hbm, hbm, vmem, vmem, vmem, hbm, vmem, vmem, vmem],
        out_specs=(hbm, hbm),
        scratch_shapes=[
            pltpu.VMEM((members, levels, fine), BF16),
            pltpu.VMEM((levels, fine), F32),
            pltpu.VMEM(conv_blocks.shape, BF16),
            pltpu.VMEM((levels, fine), F32),
            pltpu.VMEM((levels, fine), F32),
            pltpu.VMEM((part, 128), BF16),
            pltpu.VMEM((n_mem, 2 * part_tiles, part), BF16),
            pltpu.VMEM((n_col * cap, tiles), BF16),
            pltpu.VMEM((tiles, n_col * cap), BF16),
            pltpu.VMEM((n_col * 2 * cap, tiles), BF16),
            pltpu.VMEM((2 * tiles, n_col * 2 * cap), BF16),
            pltpu.VMEM((n_mem, part_tiles, feature), BF16),
            pltpu.VMEM((n_mem, feature, 2 * part_tiles), BF16),
            pltpu.VMEM((2, n_col, cap, feature), BF16),
            pltpu.VMEM((2, n_col, cap, feature), BF16),
            pltpu.VMEM((6, tiles // 2, feature), BF16),
            pltpu.VMEM((6, tiles // 2, feature), BF16),
            pltpu.VMEM((2, n_col, 2 * cap, feature), BF16),
            pltpu.VMEM((2, n_col, 2 * cap, feature), BF16),
            pltpu.VMEM((2, n_mem - 1, levels, part), BF16),
            pltpu.VMEM((2, n_mem - 1, levels, part), BF16),
            pltpu.VMEM((levels, part), F32),
            pltpu.VMEM((2, levels, part), BF16),
            pltpu.VMEM((2, n_mem - 1, levels, part), BF16),
            dma((n_mem + 2,)),
            dma((2, n_mem)),
            dma((2,)),
            dma((2,)),
            dma((2, 2)),
            dma((2, 2)),
            dma((2,)),
            dma((2,)),
            dma((2, n_mem - 1)),
            dma((2, n_mem - 1)),
            dma((2, n_mem - 1)),
            dma((2, n_mem - 1)),
        ],
        compiler_params=pltpu.CompilerParams(
            collective_id=0, has_side_effects=True, vmem_limit_bytes=48 * 1024 * 1024
        ),
        name="covariance_twice",
    )(
        neighbours,
        increment,
        ensemble,
        climate,
        restrict_dest.reshape(n_col, tiles),
        restrict_local.reshape(n_col, tiles),
        restrict_weight.reshape(1, fine),
        conv_blocks,
        pairs(interp_dest),
        pairs(interp_local),
        interp_weight,
    )


def solution(mesh):
    in_specs = (
        P(None, "col"),
        P("mem", None, "col"),
        P(None, "col"),
        P(),
        P(),
        P("col"),
        P("col", None, None, None),
        P("col", None),
        P(),
        P(),
        P(None, "col"),
    )
    out_specs = (P(None, "col"), P(None, "col"))
    return jax.shard_map(
        per_device, mesh=mesh, in_specs=in_specs, out_specs=out_specs, check_vma=False
    )
```

time: 384 us -> 98.3 us (0.26); the launches traced: 378 us -> 97.8 us
  local copies, waits for them, and re-layouts: 146 us -> 11.7 us
  blocking collectives: 97.6 us -> 0 us
  Pallas kernels: 0 us -> 83.9 us
  matrix products: 43.2 us -> 0 us
  other arithmetic: 43.5 us -> 1.64 us
  starting transfers between devices: 28.7 us -> 0 us
  waiting for transfers between devices: 17.3 us -> 0 us
    all_to_all x4 -> x0, blocking collectives: 97.6 us -> none  [the longest x2 58.8 us: sent_to_all(): return lax.all_to_all(copies, axis, split_axis=0, concat_axis=0, tiled=True)]
    pallas_call x0 -> x1, Pallas kernels: none -> 83.9 us  [per_device(): pl.pallas_call(functools.partial(kernel, cfg), out_shape=(result, result)...]
    reshape x9 -> x8, local copies, waits for them, and re-layouts: 73.7 us -> 4.1 us  [the longest x4 2.68 us: pairs(): a = a.reshape(n_col, n_mem, part_tiles, 2)]
    dot_general x18 -> x0, matrix products: 43.2 us -> none  [the longest x2 13.4 us: apply_once(): jnp.dot(fetched_small[1].reshape(feature * (coarse_local // 2), 2), spread)]
    another operation x13 -> x0, local copies, waits for them, and re-layouts: 40.7 us -> none  [the longest x2 20.1 us: apply_once(): fetched_small[1].reshape(feature * (coarse_local // 2), 2)]
    all_to_all x2 -> x0, starting transfers between devices: 24.5 us -> none  [the longest x1 13.4 us: apply_once(): lax.all_to_all(outgoing.astype(jnp.bfloat16), 'col', split_axis=0, concat...]
    reduce_sum x8 -> x0, other arithmetic: 22.7 us -> none  [the longest x2 16.1 us: apply_once(): jnp.sum(member_terms.reshape(members_here, levels, fine_local), axis=0)]
    mul x5 -> x0, other arithmetic: 13.1 us -> none  [the longest x2 9.94 us: apply_once(): product = ensemble.astype(jnp.float32) * weighted[None, :, :]]
  transfers between devices with their start and end apart: 6 -> 0, of which waited for: 4 -> 0; matrix products, arithmetic and copies ran while one was open for 12% -> 0% of each run, Pallas kernels for 0% -> 0%
where the time goes in v1:
time: 98.3 us; the launch traced here: 97.8 us
  Pallas kernels  83.9 us (85%)
  local copies, waits for them, and re-layouts  11.7 us (12%)
  other arithmetic  1.64 us (2%)
    pallas_call x1, Pallas kernels, per_device(): pl.pallas_call(functools.partial(kernel, cfg), out_shape=(result, result)...  83.9 us
    unnamed x15, local copies, waits for them, and re-layouts  7.56 us
    reshape x4, local copies, waits for them, and re-layouts, pairs(): a = a.reshape(n_col, n_mem, part_tiles, 2)  2.68 us

profile of v1, /device:TPU:1, one launch (start us, length us, event | category | flops | bytes accessed | tf_op | source)
XLA Modules:
  0.0 97.8 jit_solution(15350610099422526994)
XLA Ops:
  0.6 0.5 broadcast.3
  1.1 1.6 %reduce.3 = s32[16384]{0:T(1024)S(1)} reduce(s32[16384,1]{0,1:T(1,128)} %param.14, s32[]{:T(128)} %broadcast.3), dimensions={1}, to_apply=%param.14.reduce_sub_computation.3 | reduce | bytes 131076 | tf_op args[3]
  2.8 0.9 reshape.26.rl_ref
  3.7 1.1 %reshape.28 = s32[64,4,64,2]{2,1,0,3:T(4,128)S(1)} reshape(s32[16384,2]{0,1:T(2,128)} %param.19) | data formatting | bytes 262144 | tf_op jit(solution)/shard_map/reshape | solution.py:410
  4.8 0.2 copy.18
  5.0 0.3 reshape.29.id_ref
  5.3 1.1 %reshape.30 = s32[64,4,64,2]{2,1,0,3:T(4,128)S(1)} reshape(s32[16384,2]{0,1:T(2,128)} %param.20) | data formatting | bytes 262144 | tf_op jit(solution)/shard_map/reshape | solution.py:410
  6.4 0.2 copy.17
  6.6 0.3 reshape.31.il_ref
  6.9 0.0 copy-start
  6.9 1.0 %copy-done = f32[8,16384]{1,0:T(8,128)S(1)} copy-done((f32[8,16384]{1,0:T(8,128)S(1)}, f32[8,16384]{1,0:T(8,128)}, u32[]{:S(2)}) %copy-start) | copy-done | bytes 524312
  8.0 0.0 copy-start.1
  8.0 1.0 %copy-done.1 = f32[8,16384]{1,0:T(8,128)S(1)} copy-done((f32[8,16384]{1,0:T(8,128)S(1)}, f32[8,16384]{1,0:T(8,128)}, u32[]{:S(2)}) %copy-start.1) | copy-done | bytes 524312
  9.0 0.0 copy-start.2
  9.0 0.9 copy-done.2
  10.0 0.0 copy-start.3
  10.0 0.9 copy-done.3
  10.9 0.0 copy-start.4
  10.9 0.8 copy-done.4
  11.7 0.0 copy-start.5
  11.7 0.7 copy-done.5
  12.4 83.9 %covariance_twice.1 = (f32[8,16384]{1,0:T(8,128)S(1)}, f32[8,16384]{1,0:T(8,128)S(1)}) custom-call(s32[2,4]{1,0:T(2,128)S(1)} %copy-done.5, f32[8,16384]{1,0:T(8,128)S(1)} %copy-done, bf16[16,8,16384]{2,1,0:T(8,128)(2,1)} %ens_hbm.1, f32[8,16384]{1,0:T(8,128)S(1)} %copy-done.1, s32[64,256]{1,0:T(8,128)S(1)} %reshape.25.rd_ref, ...), custom_call_target="tpu_custom_call" | custom-call | tf_op jit(solution)/shard_map/covariance_twice/pallas_call | solution.py:418
  96.2 0.8 copy.21
  97.0 0.8 copy.22
  (1 shorter events, 0.0 us)
Async XLA Ops:
  6.9 1.0 %copy-start = (f32[8,16384]{1,0:T(8,128)S(1)}, f32[8,16384]{1,0:T(8,128)}, u32[]{:S(2)}) copy-start(f32[8,16384]{1,0:T(8,128)} %inc_ref.1) | copy-start | bytes 1572868
  8.0 1.0 %copy-start.1 = (f32[8,16384]{1,0:T(8,128)S(1)}, f32[8,16384]{1,0:T(8,128)}, u32[]{:S(2)}) copy-start(f32[8,16384]{1,0:T(8,128)} %clim_hbm.1) | copy-start | bytes 1572868
  9.0 0.9 copy-start.2
  10.0 0.9 copy-start.3
  10.9 0.8 copy-start.4
  11.7 0.7 copy-start.5

commit v2 on v1

--- a/solution.py
+++ b/solution.py
@@ -9,6 +9,7 @@
 
 TILE = 64
 CHUNK = 1024
+LAYER = 8
 F32 = jnp.float32
 BF16 = jnp.bfloat16
 MESH = pl.DeviceIdType.MESH
@@ -33,23 +34,28 @@
 def kernel(
     cfg,
     neigh_ref,
-    inc_ref,
+    inc_hbm,
     ens_hbm,
     clim_hbm,
+    rd_hbm,
+    rl_hbm,
+    rw_hbm,
+    conv_hbm,
+    id_hbm,
+    il_hbm,
+    iw_hbm,
+    result_ref,
+    inc_ref,
+    ens_ref,
+    clim_ref,
     rd_ref,
     rl_ref,
     rw_ref,
-    conv_hbm,
+    conv_ref,
     id_ref,
     il_ref,
     iw_ref,
-    once_hbm,
-    twice_hbm,
-    ens_ref,
-    clim_ref,
-    conv_ref,
     once_ref,
-    twice_ref,
     sum_ref,
     spread_ref,
     pack_ref,
@@ -69,8 +75,8 @@
     own_ref,
     ag_send,
     ag_recv,
+    ens_sem,
     in_sem,
-    out_sem,
     a1_ssem,
     a1_rsem,
     halo_ssem,
@@ -95,31 +101,54 @@
     right = lax.rem(me + 1, n_col)
     left = lax.rem(me + n_col - 1, n_col)
 
-    def ens_load(q):
-        cols = pl.ds(q * part, part)
-        return pltpu.make_async_copy(
-            ens_hbm.at[:, :, cols], ens_ref.at[:, :, cols], in_sem.at[q]
-        )
-
-    for q in range(n_mem):
-        ens_load(q).start()
-    clim_load = pltpu.make_async_copy(clim_hbm, clim_ref, in_sem.at[n_mem])
-    clim_load.start()
-    conv_load = pltpu.make_async_copy(conv_hbm, conv_ref, in_sem.at[n_mem + 1])
-    conv_load.start()
+    layers = n_col // LAYER
+    my_layer = me // LAYER
+    my_place = lax.rem(me, LAYER)
+    far_first = sorted(range(layers), key=lambda dz: -min(dz, layers - dz))
 
     barrier = pltpu.get_barrier_semaphore()
-
-    @pl.loop(1, n_col)
-    def _(i):
-        pl.semaphore_signal(
-            barrier, inc=1, device_id=(my_mem, lax.rem(me + i, n_col)), device_id_type=MESH
-        )
+    for dz in far_first:
+
+        @pl.loop(0 if dz else 1, LAYER)
+        def _(i, dz=dz):
+            peer = lax.rem(my_layer + dz, layers) * LAYER + lax.rem(my_place + i, LAYER)
+            pl.semaphore_signal(
+                barrier, inc=1, device_id=(my_mem, peer), device_id_type=MESH
+            )
 
     for i in range(1, n_mem):
         pl.semaphore_signal(
             barrier, inc=1, device_id=(lax.rem(my_mem + i, n_mem), me), device_id_type=MESH
         )
+
+    def ens_load(q):
+        cols = pl.ds(q * part, part)
+        return pltpu.make_async_copy(
+            ens_hbm.at[:, :, cols], ens_ref.at[:, :, cols], ens_sem.at[q]
+        )
+
+    loads = [
+        pltpu.make_async_copy(src, dst, in_sem.at[i])
+        for i, (src, dst) in enumerate(
+            (
+                (rd_hbm, rd_ref),
+                (rw_hbm, rw_ref),
+                (inc_hbm, inc_ref),
+                (rl_hbm, rl_ref),
+                (id_hbm, id_ref),
+                (il_hbm, il_ref),
+                (conv_hbm, conv_ref),
+                (iw_hbm, iw_ref),
+                (clim_hbm, clim_ref),
+            )
+        )
+    ]
+    for load in loads[:3]:
+        load.start()
+    for q in range(n_mem):
+        ens_load(q).start()
+    for load in loads[3:]:
+        load.start()
 
     rows = 512
 
@@ -129,7 +158,11 @@
         at = pl.ds(pl.multiple_of(c * rows, rows), rows)
         sum_ref[at, :] = ones_where((r >> 6) == iota((rows, 128), 1))
 
-    owner = rd_ref[pl.ds(me, 1), :]
+    half = tiles // 2
+    loads[0].wait()
+    owner = jnp.concatenate(
+        [rd_ref[pl.ds(2 * me, 1), :], rd_ref[pl.ds(2 * me + 1, 1), :]], axis=1
+    )
     slot_row = iota((slots1, tiles), 0)
     named = slot_row // cap == owner
     before = dot(
@@ -153,63 +186,87 @@
         acc = lax.fori_loop(0, part // CHUNK, body, jnp.zeros((feature, 128), F32))
         partial_ref[q] = acc.T[:part_tiles].astype(BF16)
 
-    def all_to_all(src, dst, ssem, rsem):
-        @pl.loop(1, n_col)
-        def _(i):
-            peer = lax.rem(me + i, n_col)
-            pltpu.make_async_remote_copy(
-                src_ref=src.at[peer],
-                dst_ref=dst.at[me],
-                send_sem=ssem,
-                recv_sem=rsem,
-                device_id=(my_mem, peer),
-                device_id_type=MESH,
-            ).start()
-
+    def all_to_all(block, src, dst, ssem, rsem):
+        for dz in far_first:
+            layer = lax.rem(my_layer + dz, layers)
+            src[pl.ds(layer * LAYER, LAYER)] = block(layer)
+
+            def send(i, carry, dz=dz, layer=layer):
+                peer = layer * LAYER + lax.rem(my_place + 4 + i, LAYER)
+                pltpu.make_async_remote_copy(
+                    src_ref=src.at[peer],
+                    dst_ref=dst.at[me],
+                    send_sem=ssem,
+                    recv_sem=rsem,
+                    device_id=(my_mem, peer),
+                    device_id_type=MESH,
+                ).start()
+                return carry
+
+            if dz:
+                lax.fori_loop(0, LAYER, send, 0, unroll=True)
+            else:
+                lax.fori_loop(0, 4, send, 0, unroll=True)
+                lax.fori_loop(5, LAYER, send, 0, unroll=True)
         dst[me] = src[me]
 
     def wait_blocks(ref, sem):
         some = ref.at[pl.ds(0, n_col - 1)]
         pltpu.make_async_copy(some, some, sem).wait()
 
-    def build_unpack():
-        spread = ones_where(iota((n_col, slots1), 0) == iota((n_col, slots1), 1) // cap)
-        mine = dot_tn(ones_where(rd_ref[...] == me), spread)
-        local = dot_tn(rl_ref[...].astype(F32).astype(BF16), spread)
-        before = dot(
-            ones_where(iota((tiles, tiles), 1) < iota((tiles, tiles), 0)), mine.astype(BF16)
-        )
-        slot = (iota((tiles, slots1), 1) % cap).astype(F32)
+    def nodes_of(mask, local, group, groups, width, start, size, many):
+        def halves(values):
+            found = []
+            for g in group:
+                column = iota((values.shape[0], width), 1) + start
+                spread = ones_where(
+                    iota((values.shape[0], width), 0) == column // size * groups + g
+                )
+                found.append(dot_tn(values, spread))
+            return jnp.concatenate(found, axis=0)
+
+        mine = halves(mask)
+        names = halves(local)
+        lower = ones_where(iota((many, many), 1) < iota((many, many), 0))
+        before = dot(lower, mine.astype(BF16))
+        slot = ((iota((many, width), 1) + start) % size).astype(F32)
         hit = jnp.where(before == slot, mine, 0.0)
-        node = jnp.sum(hit * local, axis=0, keepdims=True)
+        node = jnp.sum(hit * names, axis=0, keepdims=True)
         filled = jnp.sum(hit, axis=0, keepdims=True)
         node = jnp.where(filled > 0.5, node, -1.0)
-        unpack_ref[...] = ones_where(iota((tiles, slots1), 0).astype(F32) == node)
+        return jnp.where(iota((tiles, width), 0).astype(F32) == node, 1.0, 0.0)
+
+    def build_unpack():
+        loads[3].wait()
+        unpack_ref[...] = nodes_of(
+            ones_where(rd_ref[...] == me),
+            rl_ref[...].astype(F32).astype(BF16),
+            (0, 1),
+            2,
+            slots1,
+            0,
+            cap,
+            tiles,
+        ).astype(BF16)
 
     def build_gather():
         width = 256
-        pairs = 2 * tiles
+        loads[4].wait()
+        loads[5].wait()
         mask = ones_where(id_ref[...] == me)
-        nodes = il_ref[...].astype(F32).astype(BF16)
-        lower = ones_where(iota((pairs, pairs), 1) < iota((pairs, pairs), 0))
+        local = il_ref[...].astype(F32).astype(BF16)
         for b in range(slots2 // width):
-            column = iota((n_col, width), 1) + b * width
-            spread = ones_where(iota((n_col, width), 0) == column // cap2)
-            mine = dot_tn(mask, spread)
-            local = dot_tn(nodes, spread)
-            before = dot(lower, mine.astype(BF16))
-            slot = ((iota((pairs, width), 1) + b * width) % cap2).astype(F32)
-            hit = jnp.where(before == slot, mine, 0.0)
-            node = jnp.sum(hit * local, axis=0, keepdims=True)
-            filled = jnp.sum(hit, axis=0, keepdims=True)
-            node = jnp.where(filled > 0.5, node, -1.0)
-            block = jnp.where(iota((tiles, width), 0).astype(F32) == node, 1.0, 0.0)
+            block = nodes_of(
+                mask, local, (0, 2, 1, 3), 4, width, b * width, cap2, 2 * tiles
+            )
             gather_ref[pl.ds(b * width, width), :] = block.T.astype(BF16)
 
     def build_choose():
         width = 256
         pairs = 2 * tiles
-        target = id_ref[pl.ds(me, 1), :]
+        target = jnp.concatenate(
+            [id_ref[pl.ds(4 * me + g, 1), :] for g in (0, 2, 1, 3)], axis=1
+        )
         upper = ones_where(iota((pairs, pairs), 0) < iota((pairs, pairs), 1))
         for b in range(slots2 // width):
             slot_row = iota((width, pairs), 0) + b * width
@@ -245,22 +302,24 @@
             total += ens_ref[m, :, cols].astype(F32) * interp[m * levels : (m + 1) * levels]
         return total
 
-    def result_store(ref, hbm, q, sem):
-        cols = pl.ds(pl.multiple_of(q * part, part), part)
-        return pltpu.make_async_copy(ref.at[:, cols], hbm.at[:, cols], sem)
-
     for app in range(2):
         state_ref = inc_ref if app == 0 else once_ref
-        new_ref, new_hbm = (once_ref, once_hbm) if app == 0 else (twice_ref, twice_hbm)
         if app == 0:
+            loads[1].wait()
+            loads[2].wait()
             for q in range(n_mem):
                 ens_load(q).wait()
                 restrict(state_ref, q)
-        outgoing = dot(pack_ref[...], partial_ref[...].reshape(tiles, feature))
-        a1_send[app] = outgoing.reshape(n_col, cap, feature).astype(BF16)
+        partial = partial_ref[...].reshape(tiles, feature)
+
+        def outgoing(layer):
+            rows = LAYER * cap
+            at = pl.ds(pl.multiple_of(layer * rows, rows), rows)
+            return dot(pack_ref[at, :], partial).reshape(LAYER, cap, feature).astype(BF16)
+
         if app == 0:
             pl.semaphore_wait(barrier, n_col - 1 + n_mem - 1)
-        all_to_all(a1_send.at[app], a1_recv.at[app], a1_ssem.at[app], a1_rsem.at[app])
+        all_to_all(outgoing, a1_send.at[app], a1_recv.at[app], a1_ssem.at[app], a1_rsem.at[app])
         if app == 0:
             build_unpack()
         wait_blocks(a1_recv.at[app], a1_rsem.at[app])
@@ -282,7 +341,7 @@
             halos.append(halo)
         if app == 0:
             build_gather()
-            conv_load.wait()
+            loads[6].wait()
         for halo in halos:
             halo.wait_recv()
         nodes = []
@@ -295,19 +354,28 @@
                 term = dot(conv_ref[b, k], ext_ref[jnp.minimum(block, 5)])
                 total = term if total is None else total + term
             nodes.append(total.astype(BF16))
-        replies = dot(gather_ref[...], jnp.concatenate(nodes, axis=0))
-        a2_send[app] = replies.astype(BF16).reshape(n_col, cap2, feature)
-        all_to_all(a2_send.at[app], a2_recv.at[app], a2_ssem.at[app], a2_rsem.at[app])
+        nodes = jnp.concatenate(nodes, axis=0)
+
+        def replies(layer):
+            rows = LAYER * cap2
+            at = pl.ds(pl.multiple_of(layer * rows, rows), rows)
+            return dot(gather_ref[at, :], nodes).astype(BF16).reshape(LAYER, cap2, feature)
+
+        all_to_all(replies, a2_send.at[app], a2_recv.at[app], a2_ssem.at[app], a2_rsem.at[app])
         if app == 0:
             build_choose()
+            loads[7].wait()
             build_spread()
-            clim_load.wait()
+            loads[8].wait()
         wait_blocks(a2_recv.at[app], a2_rsem.at[app])
         answers = a2_recv[app].reshape(slots2, feature)
         fetched = dot(choose_ref[...], answers)
         for q in range(n_mem):
-            at = q * 2 * part_tiles
-            value_ref[q] = fetched[at : at + 2 * part_tiles].T.astype(BF16)
+            at = q * part_tiles
+            value_ref[q] = jnp.concatenate(
+                [fetched[at : at + part_tiles], fetched[tiles + at : tiles + at + part_tiles]],
+                axis=0,
+            ).T.astype(BF16)
 
         scatters = []
         for i in (2, 1, 3):
@@ -360,12 +428,12 @@
             else:
                 summed = ag_send[app]
             cols = pl.ds(pl.multiple_of(q * part, part), part)
-            new_ref[:, cols] = (
-                clim_ref[:, cols] * state_ref[:, cols] + summed.astype(F32) * scale
-            )
-            result_store(new_ref, new_hbm, q, out_sem.at[app, i]).start()
+            result_ref[app, :, cols] = summed
             if app == 0:
-                restrict(new_ref, q)
+                once_ref[:, cols] = (
+                    clim_ref[:, cols] * inc_ref[:, cols] + summed.astype(F32) * scale
+                )
+                restrict(once_ref, q)
         for copy in scatters:
             copy.wait_send()
         for copy in gathers.values():
@@ -376,10 +444,6 @@
     for app in range(2):
         wait_blocks(a1_send.at[app], a1_ssem.at[app])
         wait_blocks(a2_send.at[app], a2_ssem.at[app])
-        new_ref, new_hbm = (once_ref, once_hbm) if app == 0 else (twice_ref, twice_hbm)
-        for i in range(n_mem):
-            q = lax.rem(my_mem + n_mem - i, n_mem)
-            result_store(new_ref, new_hbm, q, out_sem.at[app, i]).wait()
 
 
 def per_device(
@@ -406,25 +470,31 @@
     scale = 1.0 / (members * n_mem - 1)
     cfg = (n_col, n_mem, members, levels, fine, cap, scale)
 
+    blocks = n_col * tiles // 128
+
     def pairs(a):
-        a = a.reshape(n_col, n_mem, part_tiles, 2)
-        return a.transpose(0, 1, 3, 2).reshape(n_col, 2 * tiles)
+        return a.T.reshape(2, blocks, 128).transpose(1, 0, 2).reshape(2 * blocks, 128)
 
     vmem = pl.BlockSpec(memory_space=pltpu.VMEM)
     smem = pl.BlockSpec(memory_space=pltpu.SMEM)
     hbm = pl.BlockSpec(memory_space=pl.ANY)
     dma = pltpu.SemaphoreType.DMA
-    result = jax.ShapeDtypeStruct((levels, fine), F32)
-    return pl.pallas_call(
+    sums = pl.pallas_call(
         functools.partial(kernel, cfg),
-        out_shape=(result, result),
-        in_specs=[smem, vmem, hbm, hbm, vmem, vmem, vmem, hbm, vmem, vmem, vmem],
-        out_specs=(hbm, hbm),
+        out_shape=jax.ShapeDtypeStruct((2, levels, fine), BF16),
+        in_specs=[smem] + [hbm] * 10,
+        out_specs=vmem,
         scratch_shapes=[
+            pltpu.VMEM((levels, fine), F32),
             pltpu.VMEM((members, levels, fine), BF16),
             pltpu.VMEM((levels, fine), F32),
+            pltpu.VMEM((blocks, 128), jnp.int32),
+            pltpu.VMEM((blocks, 128), jnp.int32),
+            pltpu.VMEM((1, fine), F32),
             pltpu.VMEM(conv_blocks.shape, BF16),
-            pltpu.VMEM((levels, fine), F32),
+            pltpu.VMEM((2 * blocks, 128), jnp.int32),
+            pltpu.VMEM((2 * blocks, 128), jnp.int32),
+            pltpu.VMEM((2, fine), F32),
             pltpu.VMEM((levels, fine), F32),
             pltpu.VMEM((part, 128), BF16),
             pltpu.VMEM((n_mem, 2 * part_tiles, part), BF16),
@@ -445,8 +515,8 @@
             pltpu.VMEM((levels, part), F32),
             pltpu.VMEM((2, levels, part), BF16),
             pltpu.VMEM((2, n_mem - 1, levels, part), BF16),
-            dma((n_mem + 2,)),
-            dma((2, n_mem)),
+            dma((n_mem,)),
+            dma((9,)),
             dma((2,)),
             dma((2,)),
             dma((2, 2)),
@@ -459,7 +529,7 @@
             dma((2, n_mem - 1)),
         ],
         compiler_params=pltpu.CompilerParams(
-            collective_id=0, has_side_effects=True, vmem_limit_bytes=48 * 1024 * 1024
+            collective_id=0, has_side_effects=True, vmem_limit_bytes=60 * 1024 * 1024
         ),
         name="covariance_twice",
     )(
@@ -467,14 +537,17 @@
         increment,
         ensemble,
         climate,
-        restrict_dest.reshape(n_col, tiles),
-        restrict_local.reshape(n_col, tiles),
+        restrict_dest.reshape(blocks, 128),
+        restrict_local.reshape(blocks, 128),
         restrict_weight.reshape(1, fine),
         conv_blocks,
         pairs(interp_dest),
         pairs(interp_local),
         interp_weight,
     )
+    once = climate * increment + sums[0].astype(F32) * scale
+    twice = climate * once + sums[1].astype(F32) * scale
+    return once, twice
 
 
 def solution(mesh):

time: 98.3 us -> 83.2 us (0.85)
  local copies, waits for them, and re-layouts: 11.7 us -> 0.01 us
  Pallas kernels: 83.9 us -> 80.3 us
    unnamed x15 -> x4, local copies, waits for them, and re-layouts: 7.56 us -> 0.01 us
    reshape x8 -> x0, local copies, waits for them, and re-layouts: 4.1 us -> none  [the longest x4 2.68 us: pairs(): a = a.reshape(n_col, n_mem, part_tiles, 2)]
    pallas_call x1, Pallas kernels: 83.9 us -> 80.3 us  [per_device(): pl.pallas_call(functools.partial(kernel, cfg), out_shape=jax.ShapeDtypeSt...]
    add x0 -> x1, other arithmetic: none -> 2.13 us  [per_device(): twice = climate * once + sums[1].astype(F32) * scale]
    unnamed x1 -> x0, other arithmetic: 1.64 us -> none
where the time goes in v2:
time: 83.2 us; the launch traced here: 83.1 us
  Pallas kernels  80.3 us (97%)
  other arithmetic  2.13 us (3%)
    pallas_call x1, Pallas kernels, per_device(): pl.pallas_call(functools.partial(kernel, cfg), out_shape=jax.ShapeDtypeSt...  80.3 us
    add x1, other arithmetic, per_device(): twice = climate * once + sums[1].astype(F32) * scale  2.13 us

profile of v2, /device:TPU:1, one launch (start us, length us, event | category | flops | bytes accessed | tf_op | source)
XLA Modules:
  0.0 83.1 jit_solution(16467660094650836641)
XLA Ops:
  0.6 0.0 copy-start
  0.6 0.0 copy-start.1
  0.7 80.3 %covariance_twice.1 = bf16[2,8,16384]{2,1,0:T(8,128)(2,1)} custom-call(s32[2,4]{1,0:T(2,128)} %neigh_ref.1, f32[8,16384]{1,0:T(8,128)} %inc_hbm.1, bf16[16,8,16384]{2,1,0:T(8,128)(2,1)} %ens_hbm.1, f32[8,16384]{1,0:T(8,128)} %clim_hbm.1, s32[128,128]{1,0:T(8,128)} %bitcast.24, s32[128,128]{1,0:T(8,128)} %bitcast.25, f32[1,16384]{1,0:T(1,128)} %bitcast.26, ...), custom_call_target="tpu_custom_call" | custom-call | tf_op jit(solution)/shard_map/covariance_twice/pallas_call | solution.py:482
  81.0 0.0 copy-done
  81.0 0.0 copy-done.1
  81.0 2.1 %bitcast_add_fusion = (f32[8,16384]{1,0:T(8,128)}, f32[8,16384]{1,0:T(8,128)}) fusion(f32[8,16384]{1,0:T(8,128)S(1)} %copy-done, bf16[2,8,16384]{2,1,0:T(8,128)(2,1)} %covariance_twice.1, f32[8,16384]{1,0:T(8,128)S(1)} %copy-done.1), kind=kLoop, calls=%fused_computation | loop fusion | flops 1048576 | bytes 2621440 | tf_op jit(solution)/shard_map/add | solution.py:549
Async XLA Ops:
  0.6 80.3 %copy-start = (f32[8,16384]{1,0:T(8,128)S(1)}, f32[8,16384]{1,0:T(8,128)}, u32[]{:S(2)}) copy-start(f32[8,16384]{1,0:T(8,128)} %clim_hbm.1) | copy-start | bytes 1572868
  0.6 80.3 %copy-start.1 = (f32[8,16384]{1,0:T(8,128)S(1)}, f32[8,16384]{1,0:T(8,128)}, u32[]{:S(2)}) copy-start(f32[8,16384]{1,0:T(8,128)} %inc_hbm.1) | copy-start | bytes 1572868

commit v3 on v2

--- a/solution.py
+++ b/solution.py
@@ -25,6 +25,10 @@
 
 def dot_tn(a, b):
     return lax.dot_general(a, b, (((0,), (0,)), ((), ())), preferred_element_type=F32)
+
+
+def dot_nt(a, b):
+    return lax.dot_general(a, b, (((1,), (1,)), ((), ())), preferred_element_type=F32)
 
 
 def ones_where(mask):
@@ -44,7 +48,8 @@
     id_hbm,
     il_hbm,
     iw_hbm,
-    result_ref,
+    once_hbm,
+    twice_hbm,
     inc_ref,
     ens_ref,
     clim_ref,
@@ -56,6 +61,7 @@
     il_ref,
     iw_ref,
     once_ref,
+    twice_ref,
     sum_ref,
     spread_ref,
     pack_ref,
@@ -77,6 +83,7 @@
     ag_recv,
     ens_sem,
     in_sem,
+    out_sem,
     a1_ssem,
     a1_rsem,
     halo_ssem,
@@ -150,13 +157,11 @@
     for load in loads[3:]:
         load.start()
 
-    rows = 512
-
-    @pl.loop(0, part // rows)
-    def _(c):
-        r = iota((rows, 128), 0) + c * rows
-        at = pl.ds(pl.multiple_of(c * rows, rows), rows)
-        sum_ref[at, :] = ones_where((r >> 6) == iota((rows, 128), 1))
+    chunk_tiles = CHUNK // TILE
+    per = part // CHUNK
+    sum_ref[...] = ones_where(
+        (iota((chunk_tiles, CHUNK), 1) >> 6) == iota((chunk_tiles, CHUNK), 0)
+    )
 
     half = tiles // 2
     loads[0].wait()
@@ -170,21 +175,16 @@
     )
     pack_ref[...] = ones_where(named & (before == (slot_row % cap).astype(F32)))
 
-    def restrict(state_ref, q):
-        base = q * part
-
-        def body(c, acc):
-            off = pl.multiple_of(base + c * CHUNK, CHUNK)
-            cols = pl.ds(off, CHUNK)
-            w = state_ref[:, cols] * rw_ref[:, cols]
-            prod = jnp.concatenate(
-                [ens_ref[m, :, cols].astype(F32) * w for m in range(members)], axis=0
-            ).astype(BF16)
-            at = pl.ds(pl.multiple_of(c * CHUNK, CHUNK), CHUNK)
-            return acc + dot(prod, sum_ref[at, :])
-
-        acc = lax.fori_loop(0, part // CHUNK, body, jnp.zeros((feature, 128), F32))
-        partial_ref[q] = acc.T[:part_tiles].astype(BF16)
+    def columns(chunk):
+        return pl.ds(pl.multiple_of(chunk * CHUNK, CHUNK), CHUNK)
+
+    def restrict(state, chunk):
+        cols = columns(chunk)
+        w = state * rw_ref[:, cols]
+        prod = jnp.concatenate(
+            [ens_ref[m, :, cols].astype(F32) * w for m in range(members)], axis=0
+        ).astype(BF16)
+        partial_ref[chunk] = dot_nt(sum_ref[...], prod).astype(BF16)
 
     def all_to_all(block, src, dst, ssem, rsem):
         for dz in far_first:
@@ -278,38 +278,44 @@
             choose_ref[:, pl.ds(b * width, width)] = block.T.astype(BF16)
 
     def build_spread():
-        per = part // CHUNK
-
         @pl.loop(0, n_mem * per)
         def _(i):
             q = i // per
             c = lax.rem(i, per)
-            local = pl.ds(pl.multiple_of(c * CHUNK, CHUNK), CHUNK)
-            cols = pl.ds(pl.multiple_of(i * CHUNK, CHUNK), CHUNK)
             shape = (part_tiles, CHUNK)
             mask = ((iota(shape, 1) + c * CHUNK) >> 6) == iota(shape, 0)
             for k in range(2):
-                spread_ref[q, pl.ds(k * part_tiles, part_tiles), local] = jnp.where(
-                    mask, iw_ref[pl.ds(k, 1), cols], 0.0
+                spread_ref[q, pl.ds(k * part_tiles, part_tiles), columns(c)] = jnp.where(
+                    mask, iw_ref[pl.ds(k, 1), columns(i)], 0.0
                 ).astype(BF16)
 
     def member_sum(q, c):
-        off = pl.multiple_of(c * CHUNK, CHUNK)
-        interp = dot(value_ref[q], spread_ref[q, :, pl.ds(off, CHUNK)])
-        cols = pl.ds(pl.multiple_of(q * part + off, CHUNK), CHUNK)
+        interp = dot(value_ref[q], spread_ref[q, :, columns(c)])
+        cols = columns(q * per + c)
         total = ens_ref[0, :, cols].astype(F32) * interp[0:levels]
         for m in range(1, members):
             total += ens_ref[m, :, cols].astype(F32) * interp[m * levels : (m + 1) * levels]
         return total
 
+    def wait_all(ref, sem):
+        pltpu.make_async_copy(ref, ref, sem).wait()
+
     for app in range(2):
-        state_ref = inc_ref if app == 0 else once_ref
+        old_ref, new_ref, new_hbm = (
+            (inc_ref, once_ref, once_hbm) if app == 0 else (once_ref, twice_ref, twice_hbm)
+        )
         if app == 0:
             loads[1].wait()
             loads[2].wait()
             for q in range(n_mem):
                 ens_load(q).wait()
-                restrict(state_ref, q)
+
+                def first(c, carry, q=q):
+                    chunk = q * per + c
+                    restrict(inc_ref[:, columns(chunk)], chunk)
+                    return carry
+
+                lax.fori_loop(0, per, first, 0, unroll=2)
         partial = partial_ref[...].reshape(tiles, feature)
 
         def outgoing(layer):
@@ -377,73 +383,75 @@
                 axis=0,
             ).T.astype(BF16)
 
-        scatters = []
-        for i in (2, 1, 3):
-            q = lax.rem(my_mem + i, n_mem)
-
-            @pl.loop(0, part // CHUNK)
-            def _(c, i=i, q=q):
-                at = pl.ds(pl.multiple_of(c * CHUNK, CHUNK), CHUNK)
-                rs_send[app, i - 1, :, at] = member_sum(q, c).astype(BF16)
-
-            copy = pltpu.make_async_remote_copy(
-                src_ref=rs_send.at[app, i - 1],
-                dst_ref=rs_recv.at[app, i - 1],
-                send_sem=rs_ssem.at[app, i - 1],
-                recv_sem=rs_rsem.at[app, i - 1],
-                device_id=(q, me),
-                device_id_type=MESH,
-            )
-            copy.start()
-            scatters.append(copy)
-
-        @pl.loop(0, part // CHUNK)
+        @pl.loop(0, per)
         def _(c):
-            at = pl.ds(pl.multiple_of(c * CHUNK, CHUNK), CHUNK)
-            own_ref[:, at] = member_sum(my_mem, c)
-
-        for copy in scatters:
-            copy.wait_recv()
-        total = own_ref[...]
-        for i in range(n_mem - 1):
-            total += rs_recv[app, i].astype(F32)
-        ag_send[app] = total.astype(BF16)
-        gathers = {}
-        for i in (2, 1, 3):
-            copy = pltpu.make_async_remote_copy(
-                src_ref=ag_send.at[app],
-                dst_ref=ag_recv.at[app, i - 1],
-                send_sem=ag_ssem.at[app, i - 1],
-                recv_sem=ag_rsem.at[app, i - 1],
-                device_id=(lax.rem(my_mem + i, n_mem), me),
-                device_id_type=MESH,
-            )
-            copy.start()
-            gathers[i] = copy
-        for i in (0, 1, 3, 2):
-            q = lax.rem(my_mem + n_mem - i, n_mem)
-            if i:
-                gathers[i].wait_recv()
-                summed = ag_recv[app, i - 1]
-            else:
-                summed = ag_send[app]
-            cols = pl.ds(pl.multiple_of(q * part, part), part)
-            result_ref[app, :, cols] = summed
+            pieces = []
+            for i in (2, 1, 3):
+                pieces.append((i, member_sum(lax.rem(my_mem + i, n_mem), c)))
+            for i, piece in pieces:
+                rs_send[app, c, i - 1] = piece.astype(BF16)
+                pltpu.make_async_remote_copy(
+                    src_ref=rs_send.at[app, c, i - 1],
+                    dst_ref=rs_recv.at[app, c, i - 1],
+                    send_sem=rs_ssem.at[app],
+                    recv_sem=rs_rsem.at[app, c],
+                    device_id=(lax.rem(my_mem + i, n_mem), me),
+                    device_id_type=MESH,
+                ).start()
+
+        @pl.loop(0, per)
+        def _(c):
+            own_ref[c] = member_sum(my_mem, c)
+
+        @pl.loop(0, per)
+        def _(c):
+            wait_all(rs_recv.at[app, c], rs_rsem.at[app, c])
+            total = own_ref[c]
+            for i in range(n_mem - 1):
+                total += rs_recv[app, c, i].astype(F32)
+            ag_send[app, c] = total.astype(BF16)
+            for i in (2, 1, 3):
+                pltpu.make_async_remote_copy(
+                    src_ref=ag_send.at[app, c],
+                    dst_ref=ag_recv.at[app, c, i - 1],
+                    send_sem=ag_ssem.at[app],
+                    recv_sem=ag_rsem.at[app, c],
+                    device_id=(lax.rem(my_mem + i, n_mem), me),
+                    device_id_type=MESH,
+                ).start()
+
+        def finish(q, c, summed):
+            chunk = q * per + c
+            cols = columns(chunk)
+            state = clim_ref[:, cols] * old_ref[:, cols] + summed.astype(F32) * scale
+            new_ref[:, cols] = state
+            pltpu.make_async_copy(
+                new_ref.at[:, cols], new_hbm.at[:, cols], out_sem.at[app]
+            ).start()
             if app == 0:
-                once_ref[:, cols] = (
-                    clim_ref[:, cols] * inc_ref[:, cols] + summed.astype(F32) * scale
-                )
-                restrict(once_ref, q)
-        for copy in scatters:
-            copy.wait_send()
-        for copy in gathers.values():
-            copy.wait_send()
+                restrict(state, chunk)
+
+        def finish_own(c, carry):
+            finish(my_mem, c, ag_send[app, c])
+            return carry
+
+        lax.fori_loop(0, per, finish_own, 0, unroll=2)
+
+        @pl.loop(0, per)
+        def _(c):
+            wait_all(ag_recv.at[app, c], ag_rsem.at[app, c])
+            for i in (1, 3, 2):
+                finish(lax.rem(my_mem + n_mem - i, n_mem), c, ag_recv[app, c, i - 1])
+
+        wait_all(rs_send.at[app], rs_ssem.at[app])
+        wait_all(ag_recv.at[app], ag_ssem.at[app])
         for halo in halos:
             halo.wait_send()
 
     for app in range(2):
         wait_blocks(a1_send.at[app], a1_ssem.at[app])
         wait_blocks(a2_send.at[app], a2_ssem.at[app])
+        wait_all((once_ref, twice_ref)[app], out_sem.at[app])
 
 
 def per_device(
@@ -465,6 +473,7 @@
     tiles = fine // TILE
     part = fine // n_mem
     part_tiles = part // TILE
+    per = part // CHUNK
     feature = members * levels
     cap = max(2, 2 * tiles // n_col)
     scale = 1.0 / (members * n_mem - 1)
@@ -475,15 +484,15 @@
     def pairs(a):
         return a.T.reshape(2, blocks, 128).transpose(1, 0, 2).reshape(2 * blocks, 128)
 
-    vmem = pl.BlockSpec(memory_space=pltpu.VMEM)
     smem = pl.BlockSpec(memory_space=pltpu.SMEM)
     hbm = pl.BlockSpec(memory_space=pl.ANY)
     dma = pltpu.SemaphoreType.DMA
-    sums = pl.pallas_call(
+    result = jax.ShapeDtypeStruct((levels, fine), F32)
+    return pl.pallas_call(
         functools.partial(kernel, cfg),
-        out_shape=jax.ShapeDtypeStruct((2, levels, fine), BF16),
+        out_shape=(result, result),
         in_specs=[smem] + [hbm] * 10,
-        out_specs=vmem,
+        out_specs=(hbm, hbm),
         scratch_shapes=[
             pltpu.VMEM((levels, fine), F32),
             pltpu.VMEM((members, levels, fine), BF16),
@@ -496,13 +505,14 @@
             pltpu.VMEM((2 * blocks, 128), jnp.int32),
             pltpu.VMEM((2, fine), F32),
             pltpu.VMEM((levels, fine), F32),
-            pltpu.VMEM((part, 128), BF16),
+            pltpu.VMEM((levels, fine), F32),
+            pltpu.VMEM((CHUNK // TILE, CHUNK), BF16),
             pltpu.VMEM((n_mem, 2 * part_tiles, part), BF16),
             pltpu.VMEM((n_col * cap, tiles), BF16),
             pltpu.VMEM((tiles, n_col * cap), BF16),
             pltpu.VMEM((n_col * 2 * cap, tiles), BF16),
             pltpu.VMEM((2 * tiles, n_col * 2 * cap), BF16),
-            pltpu.VMEM((n_mem, part_tiles, feature), BF16),
+            pltpu.VMEM((fine // CHUNK, CHUNK // TILE, feature), BF16),
             pltpu.VMEM((n_mem, feature, 2 * part_tiles), BF16),
             pltpu.VMEM((2, n_col, cap, feature), BF16),
             pltpu.VMEM((2, n_col, cap, feature), BF16),
@@ -510,23 +520,24 @@
             pltpu.VMEM((6, tiles // 2, feature), BF16),
             pltpu.VMEM((2, n_col, 2 * cap, feature), BF16),
             pltpu.VMEM((2, n_col, 2 * cap, feature), BF16),
-            pltpu.VMEM((2, n_mem - 1, levels, part), BF16),
-            pltpu.VMEM((2, n_mem - 1, levels, part), BF16),
-            pltpu.VMEM((levels, part), F32),
-            pltpu.VMEM((2, levels, part), BF16),
-            pltpu.VMEM((2, n_mem - 1, levels, part), BF16),
+            pltpu.VMEM((2, per, n_mem - 1, levels, CHUNK), BF16),
+            pltpu.VMEM((2, per, n_mem - 1, levels, CHUNK), BF16),
+            pltpu.VMEM((per, levels, CHUNK), F32),
+            pltpu.VMEM((2, per, levels, CHUNK), BF16),
+            pltpu.VMEM((2, per, n_mem - 1, levels, CHUNK), BF16),
             dma((n_mem,)),
             dma((9,)),
             dma((2,)),
             dma((2,)),
+            dma((2,)),
             dma((2, 2)),
             dma((2, 2)),
             dma((2,)),
             dma((2,)),
-            dma((2, n_mem - 1)),
-            dma((2, n_mem - 1)),
-            dma((2, n_mem - 1)),
-            dma((2, n_mem - 1)),
+            dma((2,)),
+            dma((2, per)),
+            dma((2,)),
+            dma((2, per)),
         ],
         compiler_params=pltpu.CompilerParams(
             collective_id=0, has_side_effects=True, vmem_limit_bytes=60 * 1024 * 1024
@@ -545,9 +556,6 @@
         pairs(interp_local),
         interp_weight,
     )
-    once = climate * increment + sums[0].astype(F32) * scale
-    twice = climate * once + sums[1].astype(F32) * scale
-    return once, twice
 
 
 def solution(mesh):

time: 83.2 us -> 76.5 us (0.919)
  Pallas kernels: 80.3 us -> 71.9 us
  local copies, waits for them, and re-layouts: 0.01 us -> 3.74 us
  other arithmetic: 2.13 us -> 0 us
    pallas_call x1, Pallas kernels: 80.3 us -> 71.9 us  [per_device(): pl.pallas_call(functools.partial(kernel, cfg), out_shape=(result, result)...]
    unnamed x4 -> x2, local copies, waits for them, and re-layouts: 0.01 us -> 3.74 us
    add x1 -> x0, other arithmetic: 2.13 us -> none  [per_device(): twice = climate * once + sums[1].astype(F32) * scale]
where the time goes in v3:
time: 76.5 us; the launch traced here: 76.3 us
  Pallas kernels  71.9 us (94%)
  local copies, waits for them, and re-layouts  3.74 us (5%)
    pallas_call x1, Pallas kernels, per_device(): pl.pallas_call(functools.partial(kernel, cfg), out_shape=(result, result)...  71.9 us
    unnamed x2, local copies, waits for them, and re-layouts  3.74 us

profile of v3, /device:TPU:1, one launch (start us, length us, event | category | flops | bytes accessed | tf_op | source)
XLA Modules:
  0.0 76.3 jit_solution(3240324751238201668)
XLA Ops:
  0.6 71.9 %covariance_twice.1 = (f32[8,16384]{1,0:T(8,128)}, f32[8,16384]{1,0:T(8,128)}) custom-call(s32[2,4]{1,0:T(2,128)} %neigh_ref.1, f32[8,16384]{1,0:T(8,128)} %inc_hbm.1, bf16[16,8,16384]{2,1,0:T(8,128)(2,1)} %ens_hbm.1, f32[8,16384]{1,0:T(8,128)} %clim_hbm.1, s32[128,128]{1,0:T(8,128)} %bitcast.19, s32[128,128]{1,0:T(8,128)} %bitcast.20, f32[1,16384]{1,0:T(1,128)} %bitcast.21, ...), custom_call_target="tpu_custom_call" | custom-call | tf_op jit(solution)/shard_map/covariance_twice/pallas_call | solution.py:491
  72.6 1.9 %copy.17 = f32[8,16384]{1,0:T(8,128)} copy(f32[8,16384]{1,0:T(8,128)} %get-tuple-element.4) | data formatting | bytes 1048576
  74.4 1.9 %copy.18 = f32[8,16384]{1,0:T(8,128)} copy(f32[8,16384]{1,0:T(8,128)} %get-tuple-element.5) | data formatting | bytes 1048576

commit v4 on v3

--- a/solution.py
+++ b/solution.py
@@ -197,7 +197,7 @@
                     src_ref=src.at[peer],
                     dst_ref=dst.at[me],
                     send_sem=ssem,
-                    recv_sem=rsem,
+                    recv_sem=rsem.at[my_layer],
                     device_id=(my_mem, peer),
                     device_id_type=MESH,
                 ).start()
@@ -213,6 +213,18 @@
     def wait_blocks(ref, sem):
         some = ref.at[pl.ds(0, n_col - 1)]
         pltpu.make_async_copy(some, some, sem).wait()
+
+    def summed_layers(matrix_ref, recv, rsem):
+        total = None
+        rows = LAYER * recv.shape[1]
+        for dz in reversed(far_first):
+            layer = lax.rem(my_layer + dz, layers)
+            some = recv.at[pl.ds(layer * LAYER, LAYER if dz else LAYER - 1)]
+            pltpu.make_async_copy(some, some, rsem.at[layer]).wait()
+            blocks = recv[pl.ds(layer * LAYER, LAYER)].astype(F32)
+            term = dot(matrix_ref[layer], blocks.reshape(rows, feature).astype(BF16))
+            total = term if total is None else total + term
+        return total
 
     def nodes_of(mask, local, group, groups, width, start, size, many):
         def halves(values):
@@ -238,7 +250,7 @@
 
     def build_unpack():
         loads[3].wait()
-        unpack_ref[...] = nodes_of(
+        found = nodes_of(
             ones_where(rd_ref[...] == me),
             rl_ref[...].astype(F32).astype(BF16),
             (0, 1),
@@ -248,6 +260,9 @@
             cap,
             tiles,
         ).astype(BF16)
+        rows = LAYER * cap
+        for layer in range(layers):
+            unpack_ref[layer] = found[:, layer * rows : (layer + 1) * rows]
 
     def build_gather():
         width = 256
@@ -262,7 +277,7 @@
             gather_ref[pl.ds(b * width, width), :] = block.T.astype(BF16)
 
     def build_choose():
-        width = 256
+        width = LAYER * cap2
         pairs = 2 * tiles
         target = jnp.concatenate(
             [id_ref[pl.ds(4 * me + g, 1), :] for g in (0, 2, 1, 3)], axis=1
@@ -275,7 +290,7 @@
             block = jnp.where(
                 named & (before == (slot_row % cap2).astype(F32)), 1.0, 0.0
             )
-            choose_ref[:, pl.ds(b * width, width)] = block.T.astype(BF16)
+            choose_ref[b] = block.T.astype(BF16)
 
     def build_spread():
         @pl.loop(0, n_mem * per)
@@ -328,10 +343,8 @@
         all_to_all(outgoing, a1_send.at[app], a1_recv.at[app], a1_ssem.at[app], a1_rsem.at[app])
         if app == 0:
             build_unpack()
-        wait_blocks(a1_recv.at[app], a1_rsem.at[app])
         ext_ref = ext_first if app == 0 else ext_second
-        incoming = a1_recv[app].astype(F32).reshape(slots1, feature).astype(BF16)
-        coarse = dot(unpack_ref[...], incoming).astype(BF16)
+        coarse = summed_layers(unpack_ref, a1_recv.at[app], a1_rsem.at[app]).astype(BF16)
         ext_ref[2:4] = coarse.reshape(2, tiles // 2, feature)
         halos = []
         for side, peer, at in ((0, right, 0), (1, left, 4)):
@@ -352,14 +365,14 @@
             halo.wait_recv()
         nodes = []
         for b in range(2):
-            total = None
+            picked = []
             for k in range(4):
                 block = lax.rem(
                     neigh_ref[b, k] - (me - 1) * 2 + 4 * n_col, 2 * n_col
                 )
-                term = dot(conv_ref[b, k], ext_ref[jnp.minimum(block, 5)])
-                total = term if total is None else total + term
-            nodes.append(total.astype(BF16))
+                picked.append(ext_ref[jnp.minimum(block, 5)])
+            blocks = jnp.concatenate([conv_ref[b, k] for k in range(4)], axis=1)
+            nodes.append(dot(blocks, jnp.concatenate(picked, axis=0)).astype(BF16))
         nodes = jnp.concatenate(nodes, axis=0)
 
         def replies(layer):
@@ -373,9 +386,7 @@
             loads[7].wait()
             build_spread()
             loads[8].wait()
-        wait_blocks(a2_recv.at[app], a2_rsem.at[app])
-        answers = a2_recv[app].reshape(slots2, feature)
-        fetched = dot(choose_ref[...], answers)
+        fetched = summed_layers(choose_ref, a2_recv.at[app], a2_rsem.at[app])
         for q in range(n_mem):
             at = q * part_tiles
             value_ref[q] = jnp.concatenate(
@@ -452,6 +463,30 @@
         wait_blocks(a1_send.at[app], a1_ssem.at[app])
         wait_blocks(a2_send.at[app], a2_ssem.at[app])
         wait_all((once_ref, twice_ref)[app], out_sem.at[app])
+
+
+def result_kernel(once_in, twice_in, once_out, twice_out, once_ref, twice_ref, sem):
+    pieces = 4
+    width = once_ref.shape[1] // pieces
+    pairs = []
+    for k, (src, ref, dst) in enumerate(
+        ((once_in, once_ref, once_out), (twice_in, twice_ref, twice_out))
+    ):
+        for p in range(pieces):
+            cols = pl.ds(p * width, width)
+            pairs.append(
+                (
+                    pltpu.make_async_copy(src.at[:, cols], ref.at[:, cols], sem.at[0, k, p]),
+                    pltpu.make_async_copy(ref.at[:, cols], dst.at[:, cols], sem.at[1, k, p]),
+                )
+            )
+    for load, _ in pairs:
+        load.start()
+    for load, store in pairs:
+        load.wait()
+        store.start()
+    for _, store in pairs:
+        store.wait()
 
 
 def per_device(
@@ -488,7 +523,7 @@
     hbm = pl.BlockSpec(memory_space=pl.ANY)
     dma = pltpu.SemaphoreType.DMA
     result = jax.ShapeDtypeStruct((levels, fine), F32)
-    return pl.pallas_call(
+    once, twice = pl.pallas_call(
         functools.partial(kernel, cfg),
         out_shape=(result, result),
         in_specs=[smem] + [hbm] * 10,
@@ -509,9 +544,9 @@
             pltpu.VMEM((CHUNK // TILE, CHUNK), BF16),
             pltpu.VMEM((n_mem, 2 * part_tiles, part), BF16),
             pltpu.VMEM((n_col * cap, tiles), BF16),
-            pltpu.VMEM((tiles, n_col * cap), BF16),
+            pltpu.VMEM((n_col // LAYER, tiles, LAYER * cap), BF16),
             pltpu.VMEM((n_col * 2 * cap, tiles), BF16),
-            pltpu.VMEM((2 * tiles, n_col * 2 * cap), BF16),
+            pltpu.VMEM((n_col // LAYER, 2 * tiles, LAYER * 2 * cap), BF16),
             pltpu.VMEM((fine // CHUNK, CHUNK // TILE, feature), BF16),
             pltpu.VMEM((n_mem, feature, 2 * part_tiles), BF16),
             pltpu.VMEM((2, n_col, cap, feature), BF16),
@@ -529,11 +564,11 @@
             dma((9,)),
             dma((2,)),
             dma((2,)),
-            dma((2,)),
+            dma((2, n_col // LAYER)),
             dma((2, 2)),
             dma((2, 2)),
             dma((2,)),
-            dma((2,)),
+            dma((2, n_col // LAYER)),
             dma((2,)),
             dma((2, per)),
             dma((2,)),
@@ -556,6 +591,19 @@
         pairs(interp_local),
         interp_weight,
     )
+    return pl.pallas_call(
+        result_kernel,
+        out_shape=(result, result),
+        in_specs=[hbm, hbm],
+        out_specs=(hbm, hbm),
+        scratch_shapes=[
+            pltpu.VMEM((levels, fine), F32),
+            pltpu.VMEM((levels, fine), F32),
+            dma((2, 2, 4)),
+        ],
+        compiler_params=pltpu.CompilerParams(vmem_limit_bytes=60 * 1024 * 1024),
+        name="results",
+    )(once, twice)
 
 
 def solution(mesh):

time: 76.5 us -> 76.4 us (level)
  Pallas kernels: 71.9 us -> 75.7 us
  local copies, waits for them, and re-layouts: 3.74 us -> 0 us
    unnamed x2 -> x0, local copies, waits for them, and re-layouts: 3.74 us -> none
    pallas_call x0 -> x1, Pallas kernels: none -> 2.09 us  [per_device(): pl.pallas_call(result_kernel, out_shape=(result, result), in_specs=[hbm,...]
    pallas_call x1, Pallas kernels: 71.9 us -> 73.6 us  [per_device(): pl.pallas_call(functools.partial(kernel, cfg), out_shape=(result, result)...]
where the time goes in v4:
time: 76.4 us; the launch traced here: 76.3 us
  Pallas kernels  75.7 us (99%)
    pallas_call x1, Pallas kernels, per_device(): pl.pallas_call(functools.partial(kernel, cfg), out_shape=(result, result)...  73.6 us
    pallas_call x1, Pallas kernels, per_device(): pl.pallas_call(result_kernel, out_shape=(result, result), in_specs=[hbm,...  2.09 us

profile of v4, /device:TPU:1, one launch (start us, length us, event | category | flops | bytes accessed | tf_op | source)
XLA Modules:
  0.0 76.3 jit_solution(4327464414473928510)
XLA Ops:
  0.6 73.6 %covariance_twice.1 = (f32[8,16384]{1,0:T(8,128)}, f32[8,16384]{1,0:T(8,128)}) custom-call(s32[2,4]{1,0:T(2,128)} %neigh_ref.1, f32[8,16384]{1,0:T(8,128)} %inc_hbm.1, bf16[16,8,16384]{2,1,0:T(8,128)(2,1)} %ens_hbm.1, f32[8,16384]{1,0:T(8,128)} %clim_hbm.1, s32[128,128]{1,0:T(8,128)} %bitcast.19, s32[128,128]{1,0:T(8,128)} %bitcast.20, f32[1,16384]{1,0:T(1,128)} %bitcast.21, ...), custom_call_target="tpu_custom_call" | custom-call | tf_op jit(solution)/shard_map/covariance_twice/pallas_call | solution.py:526
  74.2 2.1 %results.1 = (f32[8,16384]{1,0:T(8,128)}, f32[8,16384]{1,0:T(8,128)}) custom-call(f32[8,16384]{1,0:T(8,128)} %get-tuple-element.4.once_in, f32[8,16384]{1,0:T(8,128)} %get-tuple-element.5.twice_in), custom_call_target="tpu_custom_call" | custom-call | tf_op jit(solution)/shard_map/results/pallas_call | solution.py:594

commit v5 on v4

--- a/solution.py
+++ b/solution.py
@@ -105,28 +105,13 @@
     slots2 = n_col * cap2
     me = lax.axis_index("col")
     my_mem = lax.axis_index("mem")
-    right = lax.rem(me + 1, n_col)
-    left = lax.rem(me + n_col - 1, n_col)
+    core = lax.rem(me, 2)
+    partner = me + 1 - 2 * core
 
     layers = n_col // LAYER
     my_layer = me // LAYER
     my_place = lax.rem(me, LAYER)
     far_first = sorted(range(layers), key=lambda dz: -min(dz, layers - dz))
-
-    barrier = pltpu.get_barrier_semaphore()
-    for dz in far_first:
-
-        @pl.loop(0 if dz else 1, LAYER)
-        def _(i, dz=dz):
-            peer = lax.rem(my_layer + dz, layers) * LAYER + lax.rem(my_place + i, LAYER)
-            pl.semaphore_signal(
-                barrier, inc=1, device_id=(my_mem, peer), device_id_type=MESH
-            )
-
-    for i in range(1, n_mem):
-        pl.semaphore_signal(
-            barrier, inc=1, device_id=(lax.rem(my_mem + i, n_mem), me), device_id_type=MESH
-        )
 
     def ens_load(q):
         cols = pl.ds(q * part, part)
@@ -154,6 +139,21 @@
         load.start()
     for q in range(n_mem):
         ens_load(q).start()
+    barrier = pltpu.get_barrier_semaphore()
+    for dz in far_first:
+
+        @pl.loop(0 if dz else 1, LAYER)
+        def _(i, dz=dz):
+            peer = lax.rem(my_layer + dz, layers) * LAYER + lax.rem(my_place + i, LAYER)
+            pl.semaphore_signal(
+                barrier, inc=1, device_id=(my_mem, peer), device_id_type=MESH
+            )
+
+    for i in range(1, n_mem):
+        pl.semaphore_signal(
+            barrier, inc=1, device_id=(lax.rem(my_mem + i, n_mem), me), device_id_type=MESH
+        )
+
     for load in loads[3:]:
         load.start()
 
@@ -186,18 +186,18 @@
         ).astype(BF16)
         partial_ref[chunk] = dot_nt(sum_ref[...], prod).astype(BF16)
 
-    def all_to_all(block, src, dst, ssem, rsem):
+    def all_to_all(ready, source, dst, ssem, rsem):
         for dz in far_first:
             layer = lax.rem(my_layer + dz, layers)
-            src[pl.ds(layer * LAYER, LAYER)] = block(layer)
+            ready(layer)
 
             def send(i, carry, dz=dz, layer=layer):
                 peer = layer * LAYER + lax.rem(my_place + 4 + i, LAYER)
                 pltpu.make_async_remote_copy(
-                    src_ref=src.at[peer],
+                    src_ref=source(peer),
                     dst_ref=dst.at[me],
                     send_sem=ssem,
-                    recv_sem=rsem.at[my_layer],
+                    recv_sem=rsem,
                     device_id=(my_mem, peer),
                     device_id_type=MESH,
                 ).start()
@@ -208,23 +208,10 @@
             else:
                 lax.fori_loop(0, 4, send, 0, unroll=True)
                 lax.fori_loop(5, LAYER, send, 0, unroll=True)
-        dst[me] = src[me]
 
     def wait_blocks(ref, sem):
         some = ref.at[pl.ds(0, n_col - 1)]
         pltpu.make_async_copy(some, some, sem).wait()
-
-    def summed_layers(matrix_ref, recv, rsem):
-        total = None
-        rows = LAYER * recv.shape[1]
-        for dz in reversed(far_first):
-            layer = lax.rem(my_layer + dz, layers)
-            some = recv.at[pl.ds(layer * LAYER, LAYER if dz else LAYER - 1)]
-            pltpu.make_async_copy(some, some, rsem.at[layer]).wait()
-            blocks = recv[pl.ds(layer * LAYER, LAYER)].astype(F32)
-            term = dot(matrix_ref[layer], blocks.reshape(rows, feature).astype(BF16))
-            total = term if total is None else total + term
-        return total
 
     def nodes_of(mask, local, group, groups, width, start, size, many):
         def halves(values):
@@ -250,19 +237,12 @@
 
     def build_unpack():
         loads[3].wait()
-        found = nodes_of(
-            ones_where(rd_ref[...] == me),
-            rl_ref[...].astype(F32).astype(BF16),
-            (0, 1),
-            2,
-            slots1,
-            0,
-            cap,
-            tiles,
-        ).astype(BF16)
-        rows = LAYER * cap
-        for layer in range(layers):
-            unpack_ref[layer] = found[:, layer * rows : (layer + 1) * rows]
+        local = rl_ref[...].astype(F32).astype(BF16)
+        for o in range(2):
+            who = lax.rem(me + core + o + n_col - 1, n_col)
+            mask = ones_where(rd_ref[...] == who)
+            found = nodes_of(mask, local, (0, 1), 2, slots1, 0, cap, tiles)
+            unpack_ref[o] = found.astype(BF16)
 
     def build_gather():
         width = 256
@@ -277,7 +257,7 @@
             gather_ref[pl.ds(b * width, width), :] = block.T.astype(BF16)
 
     def build_choose():
-        width = LAYER * cap2
+        width = 256
         pairs = 2 * tiles
         target = jnp.concatenate(
             [id_ref[pl.ds(4 * me + g, 1), :] for g in (0, 2, 1, 3)], axis=1
@@ -290,7 +270,7 @@
             block = jnp.where(
                 named & (before == (slot_row % cap2).astype(F32)), 1.0, 0.0
             )
-            choose_ref[b] = block.T.astype(BF16)
+            choose_ref[:, pl.ds(b * width, width)] = block.T.astype(BF16)
 
     def build_spread():
         @pl.loop(0, n_mem * per)
@@ -330,39 +310,48 @@
                     restrict(inc_ref[:, columns(chunk)], chunk)
                     return carry
 
-                lax.fori_loop(0, per, first, 0, unroll=2)
+                lax.fori_loop(0, per, first, 0, unroll=4)
         partial = partial_ref[...].reshape(tiles, feature)
 
-        def outgoing(layer):
-            rows = LAYER * cap
-            at = pl.ds(pl.multiple_of(layer * rows, rows), rows)
-            return dot(pack_ref[at, :], partial).reshape(LAYER, cap, feature).astype(BF16)
-
+        outgoing = dot(pack_ref[...], partial).reshape(n_col, cap, feature).astype(BF16)
+        a1_send[app, pl.ds(1, n_col)] = outgoing
+        a1_send[app, 0] = outgoing[n_col - 1]
+        a1_send[app, n_col + 1] = outgoing[0]
         if app == 0:
             pl.semaphore_wait(barrier, n_col - 1 + n_mem - 1)
-        all_to_all(outgoing, a1_send.at[app], a1_recv.at[app], a1_ssem.at[app], a1_rsem.at[app])
+
+        def two_owners(peer):
+            return a1_send.at[app, pl.ds(peer + lax.rem(peer, 2), 2)]
+
+        all_to_all(
+            lambda layer: None, two_owners, a1_recv.at[app], a1_ssem.at[app], a1_rsem.at[app]
+        )
+        a1_recv[app, me] = a1_send[app, pl.ds(me + core, 2)]
         if app == 0:
             build_unpack()
+        wait_blocks(a1_recv.at[app], a1_rsem.at[app])
         ext_ref = ext_first if app == 0 else ext_second
-        coarse = summed_layers(unpack_ref, a1_recv.at[app], a1_rsem.at[app]).astype(BF16)
-        ext_ref[2:4] = coarse.reshape(2, tiles // 2, feature)
-        halos = []
-        for side, peer, at in ((0, right, 0), (1, left, 4)):
-            halo = pltpu.make_async_remote_copy(
-                src_ref=ext_ref.at[pl.ds(2, 2)],
-                dst_ref=ext_ref.at[pl.ds(at, 2)],
-                send_sem=halo_ssem.at[app, side],
-                recv_sem=halo_rsem.at[app, side],
-                device_id=(my_mem, peer),
-                device_id_type=MESH,
-            )
-            halo.start()
-            halos.append(halo)
+
+        def coarse(o):
+            incoming = a1_recv[app, :, o].astype(F32).reshape(slots1, feature)
+            values = dot(unpack_ref[o], incoming.astype(BF16)).astype(BF16)
+            return values.reshape(2, tiles // 2, feature)
+
+        ext_ref[pl.ds(2, 2)] = coarse(1 - core)
+        halo = pltpu.make_async_remote_copy(
+            src_ref=ext_ref.at[pl.ds(2, 2)],
+            dst_ref=ext_ref.at[pl.ds(4 * core, 2)],
+            send_sem=halo_ssem.at[app],
+            recv_sem=halo_rsem.at[app],
+            device_id=(my_mem, partner),
+            device_id_type=MESH,
+        )
+        halo.start()
+        ext_ref[pl.ds(4 * core, 2)] = coarse(core)
         if app == 0:
             build_gather()
             loads[6].wait()
-        for halo in halos:
-            halo.wait_recv()
+        halo.wait_recv()
         nodes = []
         for b in range(2):
             picked = []
@@ -378,15 +367,18 @@
         def replies(layer):
             rows = LAYER * cap2
             at = pl.ds(pl.multiple_of(layer * rows, rows), rows)
-            return dot(gather_ref[at, :], nodes).astype(BF16).reshape(LAYER, cap2, feature)
-
-        all_to_all(replies, a2_send.at[app], a2_recv.at[app], a2_ssem.at[app], a2_rsem.at[app])
+            block = dot(gather_ref[at, :], nodes).astype(BF16)
+            a2_send[app, pl.ds(layer * LAYER, LAYER)] = block.reshape(LAYER, cap2, feature)
+
+        all_to_all(replies, lambda peer: a2_send.at[app, peer], a2_recv.at[app], a2_ssem.at[app], a2_rsem.at[app])
+        a2_recv[app, me] = a2_send[app, me]
         if app == 0:
             build_choose()
             loads[7].wait()
             build_spread()
             loads[8].wait()
-        fetched = summed_layers(choose_ref, a2_recv.at[app], a2_rsem.at[app])
+        wait_blocks(a2_recv.at[app], a2_rsem.at[app])
+        fetched = dot(choose_ref[...], a2_recv[app].reshape(slots2, feature))
         for q in range(n_mem):
             at = q * part_tiles
             value_ref[q] = jnp.concatenate(
@@ -456,11 +448,10 @@
 
         wait_all(rs_send.at[app], rs_ssem.at[app])
         wait_all(ag_recv.at[app], ag_ssem.at[app])
-        for halo in halos:
-            halo.wait_send()
+        halo.wait_send()
 
     for app in range(2):
-        wait_blocks(a1_send.at[app], a1_ssem.at[app])
+        wait_blocks(a1_recv.at[app], a1_ssem.at[app])
         wait_blocks(a2_send.at[app], a2_ssem.at[app])
         wait_all((once_ref, twice_ref)[app], out_sem.at[app])
 
@@ -544,13 +535,13 @@
             pltpu.VMEM((CHUNK // TILE, CHUNK), BF16),
             pltpu.VMEM((n_mem, 2 * part_tiles, part), BF16),
             pltpu.VMEM((n_col * cap, tiles), BF16),
-            pltpu.VMEM((n_col // LAYER, tiles, LAYER * cap), BF16),
+            pltpu.VMEM((2, tiles, n_col * cap), BF16),
             pltpu.VMEM((n_col * 2 * cap, tiles), BF16),
-            pltpu.VMEM((n_col // LAYER, 2 * tiles, LAYER * 2 * cap), BF16),
+            pltpu.VMEM((2 * tiles, n_col * 2 * cap), BF16),
             pltpu.VMEM((fine // CHUNK, CHUNK // TILE, feature), BF16),
             pltpu.VMEM((n_mem, feature, 2 * part_tiles), BF16),
-            pltpu.VMEM((2, n_col, cap, feature), BF16),
-            pltpu.VMEM((2, n_col, cap, feature), BF16),
+            pltpu.VMEM((2, n_col + 2, cap, feature), BF16),
+            pltpu.VMEM((2, n_col, 2, cap, feature), BF16),
             pltpu.VMEM((6, tiles // 2, feature), BF16),
             pltpu.VMEM((6, tiles // 2, feature), BF16),
             pltpu.VMEM((2, n_col, 2 * cap, feature), BF16),
@@ -564,11 +555,11 @@
             dma((9,)),
             dma((2,)),
             dma((2,)),
-            dma((2, n_col // LAYER)),
-            dma((2, 2)),
-            dma((2, 2)),
-            dma((2,)),
-            dma((2, n_col // LAYER)),
+            dma((2,)),
+            dma((2,)),
+            dma((2,)),
+            dma((2,)),
+            dma((2,)),
             dma((2,)),
             dma((2, per)),
             dma((2,)),

time: 76.4 us -> 75.5 us (0.988)
  Pallas kernels: 75.7 us -> 74.8 us
    pallas_call x1, Pallas kernels: 73.6 us -> 72.7 us  [per_device(): pl.pallas_call(functools.partial(kernel, cfg), out_shape=(result, result)...]
where the time goes in v5:
time: 75.5 us; the launch traced here: 75.4 us
  Pallas kernels  74.8 us (99%)
    pallas_call x1, Pallas kernels, per_device(): pl.pallas_call(functools.partial(kernel, cfg), out_shape=(result, result)...  72.7 us
    pallas_call x1, Pallas kernels, per_device(): pl.pallas_call(result_kernel, out_shape=(result, result), in_specs=[hbm,...  2.09 us

profile of v5, /device:TPU:1, one launch (start us, length us, event | category | flops | bytes accessed | tf_op | source)
XLA Modules:
  0.0 75.4 jit_solution(5395462130286241627)
XLA Ops:
  0.6 72.7 %covariance_twice.1 = (f32[8,16384]{1,0:T(8,128)}, f32[8,16384]{1,0:T(8,128)}) custom-call(s32[2,4]{1,0:T(2,128)} %neigh_ref.1, f32[8,16384]{1,0:T(8,128)} %inc_hbm.1, bf16[16,8,16384]{2,1,0:T(8,128)(2,1)} %ens_hbm.1, f32[8,16384]{1,0:T(8,128)} %clim_hbm.1, s32[128,128]{1,0:T(8,128)} %bitcast.19, s32[128,128]{1,0:T(8,128)} %bitcast.20, f32[1,16384]{1,0:T(1,128)} %bitcast.21, ...), custom_call_target="tpu_custom_call" | custom-call | tf_op jit(solution)/shard_map/covariance_twice/pallas_call | solution.py:517
  73.3 2.1 %results.1 = (f32[8,16384]{1,0:T(8,128)}, f32[8,16384]{1,0:T(8,128)}) custom-call(f32[8,16384]{1,0:T(8,128)} %get-tuple-element.4.once_in, f32[8,16384]{1,0:T(8,128)} %get-tuple-element.5.twice_in), custom_call_target="tpu_custom_call" | custom-call | tf_op jit(solution)/shard_map/results/pallas_call | solution.py:585

commit v6 on v3

--- a/solution.py
+++ b/solution.py
@@ -113,21 +113,6 @@
     my_place = lax.rem(me, LAYER)
     far_first = sorted(range(layers), key=lambda dz: -min(dz, layers - dz))
 
-    barrier = pltpu.get_barrier_semaphore()
-    for dz in far_first:
-
-        @pl.loop(0 if dz else 1, LAYER)
-        def _(i, dz=dz):
-            peer = lax.rem(my_layer + dz, layers) * LAYER + lax.rem(my_place + i, LAYER)
-            pl.semaphore_signal(
-                barrier, inc=1, device_id=(my_mem, peer), device_id_type=MESH
-            )
-
-    for i in range(1, n_mem):
-        pl.semaphore_signal(
-            barrier, inc=1, device_id=(lax.rem(my_mem + i, n_mem), me), device_id_type=MESH
-        )
-
     def ens_load(q):
         cols = pl.ds(q * part, part)
         return pltpu.make_async_copy(
@@ -154,6 +139,21 @@
         load.start()
     for q in range(n_mem):
         ens_load(q).start()
+    barrier = pltpu.get_barrier_semaphore()
+    for dz in far_first:
+
+        @pl.loop(0 if dz else 1, LAYER)
+        def _(i, dz=dz):
+            peer = lax.rem(my_layer + dz, layers) * LAYER + lax.rem(my_place + i, LAYER)
+            pl.semaphore_signal(
+                barrier, inc=1, device_id=(my_mem, peer), device_id_type=MESH
+            )
+
+    for i in range(1, n_mem):
+        pl.semaphore_signal(
+            barrier, inc=1, device_id=(lax.rem(my_mem + i, n_mem), me), device_id_type=MESH
+        )
+
     for load in loads[3:]:
         load.start()
 
@@ -275,7 +275,13 @@
             block = jnp.where(
                 named & (before == (slot_row % cap2).astype(F32)), 1.0, 0.0
             )
-            choose_ref[:, pl.ds(b * width, width)] = block.T.astype(BF16)
+            block = block.T.astype(BF16)
+            for q in range(n_mem):
+                for k in range(2):
+                    at = k * tiles + q * part_tiles
+                    choose_ref[q, pl.ds(k * part_tiles, part_tiles), pl.ds(b * width, width)] = (
+                        block[at : at + part_tiles]
+                    )
 
     def build_spread():
         @pl.loop(0, n_mem * per)
@@ -375,13 +381,12 @@
             loads[8].wait()
         wait_blocks(a2_recv.at[app], a2_rsem.at[app])
         answers = a2_recv[app].reshape(slots2, feature)
-        fetched = dot(choose_ref[...], answers)
-        for q in range(n_mem):
-            at = q * part_tiles
-            value_ref[q] = jnp.concatenate(
-                [fetched[at : at + part_tiles], fetched[tiles + at : tiles + at + part_tiles]],
-                axis=0,
-            ).T.astype(BF16)
+
+        def fetch(q):
+            value_ref[q] = dot(choose_ref[q], answers).T.astype(BF16)
+
+        for i in (2, 1, 3):
+            fetch(lax.rem(my_mem + i, n_mem))
 
         @pl.loop(0, per)
         def _(c):
@@ -398,6 +403,8 @@
                     device_id=(lax.rem(my_mem + i, n_mem), me),
                     device_id_type=MESH,
                 ).start()
+
+        fetch(my_mem)
 
         @pl.loop(0, per)
         def _(c):
@@ -452,6 +459,30 @@
         wait_blocks(a1_send.at[app], a1_ssem.at[app])
         wait_blocks(a2_send.at[app], a2_ssem.at[app])
         wait_all((once_ref, twice_ref)[app], out_sem.at[app])
+
+
+def result_kernel(once_in, twice_in, once_out, twice_out, once_ref, twice_ref, sem):
+    pieces = 4
+    width = once_ref.shape[1] // pieces
+    pairs = []
+    for k, (src, ref, dst) in enumerate(
+        ((once_in, once_ref, once_out), (twice_in, twice_ref, twice_out))
+    ):
+        for p in range(pieces):
+            cols = pl.ds(p * width, width)
+            pairs.append(
+                (
+                    pltpu.make_async_copy(src.at[:, cols], ref.at[:, cols], sem.at[0, k, p]),
+                    pltpu.make_async_copy(ref.at[:, cols], dst.at[:, cols], sem.at[1, k, p]),
+                )
+            )
+    for load, _ in pairs:
+        load.start()
+    for load, store in pairs:
+        load.wait()
+        store.start()
+    for _, store in pairs:
+        store.wait()
 
 
 def per_device(
@@ -488,7 +519,7 @@
     hbm = pl.BlockSpec(memory_space=pl.ANY)
     dma = pltpu.SemaphoreType.DMA
     result = jax.ShapeDtypeStruct((levels, fine), F32)
-    return pl.pallas_call(
+    once, twice = pl.pallas_call(
         functools.partial(kernel, cfg),
         out_shape=(result, result),
         in_specs=[smem] + [hbm] * 10,
@@ -511,7 +542,7 @@
             pltpu.VMEM((n_col * cap, tiles), BF16),
             pltpu.VMEM((tiles, n_col * cap), BF16),
             pltpu.VMEM((n_col * 2 * cap, tiles), BF16),
-            pltpu.VMEM((2 * tiles, n_col * 2 * cap), BF16),
+            pltpu.VMEM((n_mem, 2 * part_tiles, n_col * 2 * cap), BF16),
             pltpu.VMEM((fine // CHUNK, CHUNK // TILE, feature), BF16),
             pltpu.VMEM((n_mem, feature, 2 * part_tiles), BF16),
             pltpu.VMEM((2, n_col, cap, feature), BF16),
@@ -556,6 +587,19 @@
         pairs(interp_local),
         interp_weight,
     )
+    return pl.pallas_call(
+        result_kernel,
+        out_shape=(result, result),
+        in_specs=[hbm, hbm],
+        out_specs=(hbm, hbm),
+        scratch_shapes=[
+            pltpu.VMEM((levels, fine), F32),
+            pltpu.VMEM((levels, fine), F32),
+            dma((2, 2, 4)),
+        ],
+        compiler_params=pltpu.CompilerParams(vmem_limit_bytes=60 * 1024 * 1024),
+        name="results",
+    )(once, twice)
 
 
 def solution(mesh):

time: 76.5 us -> 74.4 us (0.973)
  local copies, waits for them, and re-layouts: 3.74 us -> 0 us
  Pallas kernels: 71.9 us -> 73.6 us
    unnamed x2 -> x0, local copies, waits for them, and re-layouts: 3.74 us -> none
    pallas_call x0 -> x1, Pallas kernels: none -> 2.09 us  [per_device(): pl.pallas_call(result_kernel, out_shape=(result, result), in_specs=[hbm,...]
where the time goes in v6:
time: 74.4 us; the launch traced here: 74.3 us
  Pallas kernels  73.6 us (99%)
    pallas_call x1, Pallas kernels, per_device(): pl.pallas_call(functools.partial(kernel, cfg), out_shape=(result, result)...  71.6 us
    pallas_call x1, Pallas kernels, per_device(): pl.pallas_call(result_kernel, out_shape=(result, result), in_specs=[hbm,...  2.09 us

profile of v6, /device:TPU:1, one launch (start us, length us, event | category | flops | bytes accessed | tf_op | source)
XLA Modules:
  0.0 74.3 jit_solution(18403381836093918483)
XLA Ops:
  0.6 71.6 %covariance_twice.1 = (f32[8,16384]{1,0:T(8,128)}, f32[8,16384]{1,0:T(8,128)}) custom-call(s32[2,4]{1,0:T(2,128)} %neigh_ref.1, f32[8,16384]{1,0:T(8,128)} %inc_hbm.1, bf16[16,8,16384]{2,1,0:T(8,128)(2,1)} %ens_hbm.1, f32[8,16384]{1,0:T(8,128)} %clim_hbm.1, s32[128,128]{1,0:T(8,128)} %bitcast.19, s32[128,128]{1,0:T(8,128)} %bitcast.20, f32[1,16384]{1,0:T(1,128)} %bitcast.21, ...), custom_call_target="tpu_custom_call" | custom-call | tf_op jit(solution)/shard_map/covariance_twice/pallas_call | solution.py:522
  72.2 2.1 %results.1 = (f32[8,16384]{1,0:T(8,128)}, f32[8,16384]{1,0:T(8,128)}) custom-call(f32[8,16384]{1,0:T(8,128)} %get-tuple-element.4.once_in, f32[8,16384]{1,0:T(8,128)} %get-tuple-element.5.twice_in), custom_call_target="tpu_custom_call" | custom-call | tf_op jit(solution)/shard_map/results/pallas_call | solution.py:590

commit v7 on v6

--- a/solution.py
+++ b/solution.py
@@ -189,7 +189,8 @@
     def all_to_all(block, src, dst, ssem, rsem):
         for dz in far_first:
             layer = lax.rem(my_layer + dz, layers)
-            src[pl.ds(layer * LAYER, LAYER)] = block(layer)
+            if block is not None:
+                src[pl.ds(layer * LAYER, LAYER)] = block(layer)
 
             def send(i, carry, dz=dz, layer=layer):
                 peer = layer * LAYER + lax.rem(my_place + 4 + i, LAYER)
@@ -324,14 +325,12 @@
                 lax.fori_loop(0, per, first, 0, unroll=2)
         partial = partial_ref[...].reshape(tiles, feature)
 
-        def outgoing(layer):
-            rows = LAYER * cap
-            at = pl.ds(pl.multiple_of(layer * rows, rows), rows)
-            return dot(pack_ref[at, :], partial).reshape(LAYER, cap, feature).astype(BF16)
+        outgoing = dot(pack_ref[...], partial)
+        a1_send[app] = outgoing.reshape(n_col, cap, feature).astype(BF16)
 
         if app == 0:
             pl.semaphore_wait(barrier, n_col - 1 + n_mem - 1)
-        all_to_all(outgoing, a1_send.at[app], a1_recv.at[app], a1_ssem.at[app], a1_rsem.at[app])
+        all_to_all(None, a1_send.at[app], a1_recv.at[app], a1_ssem.at[app], a1_rsem.at[app])
         if app == 0:
             build_unpack()
         wait_blocks(a1_recv.at[app], a1_rsem.at[app])

time: 74.4 us -> 74.1 us (level)
  no operation moved by 1% of the time
where the time goes in v7:
time: 74.1 us; the launch traced here: 74 us
  Pallas kernels  73.3 us (99%)
    pallas_call x1, Pallas kernels, per_device(): pl.pallas_call(functools.partial(kernel, cfg), out_shape=(result, result)...  71.2 us
    pallas_call x1, Pallas kernels, per_device(): pl.pallas_call(result_kernel, out_shape=(result, result), in_specs=[hbm,...  2.09 us

profile of v7, /device:TPU:1, one launch (start us, length us, event | category | flops | bytes accessed | tf_op | source)
XLA Modules:
  0.0 74.0 jit_solution(8382737385980646193)
XLA Ops:
  0.6 71.2 %covariance_twice.1 = (f32[8,16384]{1,0:T(8,128)}, f32[8,16384]{1,0:T(8,128)}) custom-call(s32[2,4]{1,0:T(2,128)} %neigh_ref.1, f32[8,16384]{1,0:T(8,128)} %inc_hbm.1, bf16[16,8,16384]{2,1,0:T(8,128)(2,1)} %ens_hbm.1, f32[8,16384]{1,0:T(8,128)} %clim_hbm.1, s32[128,128]{1,0:T(8,128)} %bitcast.19, s32[128,128]{1,0:T(8,128)} %bitcast.20, f32[1,16384]{1,0:T(1,128)} %bitcast.21, ...), custom_call_target="tpu_custom_call" | custom-call | tf_op jit(solution)/shard_map/covariance_twice/pallas_call | solution.py:521
  71.9 2.1 %results.1 = (f32[8,16384]{1,0:T(8,128)}, f32[8,16384]{1,0:T(8,128)}) custom-call(f32[8,16384]{1,0:T(8,128)} %get-tuple-element.4.once_in, f32[8,16384]{1,0:T(8,128)} %get-tuple-element.5.twice_in), custom_call_target="tpu_custom_call" | custom-call | tf_op jit(solution)/shard_map/results/pallas_call | solution.py:589
